TPU v7x, 128 devices: a whole 4x4x4 slice. The times are simulated.
128 devices in a mesh: lon: 32 (over y, z, x_hi), lat: 4 (over x_lo, core).
Axes of the slice: x: 4 (x_hi: 2, x_lo: 2; x = x_hi * 2 + x_lo), y: 4, z: 4, core: 2. Of those that a mesh axis runs over, the one named last changes fastest.
Arguments:
- spectrum: float32 [1296, 256, 512], P(None, 'lon', 'lat'), may hold values from -6 to 6
- sea_mask: int32 [256, 512], P('lon', 'lat'), may hold values 0 or 1
- transfer: bfloat16 [1296, 1296], replicated, may hold values from -0.15625 to 0.15625
- bulk_weight: float32 [5, 1296], replicated, may hold values from -0.15625 to 0.15625
- remap_cell: int32 [768, 1536, 4], P('lon', 'lat'), may hold values from 0 to 8703, as said below
- remap_weight: float32 [768, 1536, 4], P('lon', 'lat'), may hold values from 0.1 to 0.5
- ocean_u: float32 [8, 768, 1536], P(None, 'lon', 'lat'), may hold values from -6 to 6
- ocean_v: float32 [8, 768, 1536], P(None, 'lon', 'lat'), may hold values from -6 to 6
- ocean_mask: int32 [768, 1536], P('lon', 'lat'), may hold values 0 or 1
- coriolis: float32 [1536], P('lat'), may hold values from -1 to 1
Outputs:
- spectrum_out: float32 [1296, 256, 512], P(None, 'lon', 'lat')
- ocean_u_out: float32 [8, 768, 1536], P(None, 'lon', 'lat')
- ocean_v_out: float32 [8, 768, 1536], P(None, 'lon', 'lat')
Inputs may be any that keep to these rules, and one draw needn't show every extreme that they name: `remap_cell`: for ocean cell (i, j) each entry c has c // 512 between 0 and 16, and its wave latitude c % 512 lies in the same block of 128 latitude cells as j // 3.
All inputs are finite; a program needn't handle non-finite values. No bound on the sum of `sea_mask` or of `ocean_mask` on one device may be relied on, other than what follows from the above.
Results may differ from a plain program's by a relative error of at most 0.0016.
Values sent between devices are 32-bit elements; how exact they have to be, the bound alone decides.
A program may use at most 128 MiB of HBM per device.

v0:
```python
import jax
import jax.numpy as jnp
from jax import lax
from jax.sharding import PartitionSpec as P

NFREQ = 36


def passed_along(value, axis, steps):
    count = lax.axis_size(axis)
    first, last = (max(0, -steps), min(count, count - steps))
    return lax.ppermute(value, axis, [(source, source + steps) for source in range(first, last)])


def with_halo(array, sides, width, wrap):
    for axis, dim in sides:
        count, length = (lax.axis_size(axis), array.shape[dim])
        up = [(i, (i + 1) % count) for i in range(count if wrap else count - 1)]
        down = [(j, i) for i, j in up]
        last = lax.slice_in_dim(array, length - width, length, axis=dim)
        first = lax.slice_in_dim(array, 0, width, axis=dim)
        before = lax.ppermute(last, axis, up)
        after = lax.ppermute(first, axis, down)
        array = jnp.concatenate([before, array, after], axis=dim)
    return array


def courant(components, freqs):
    index = jnp.arange(components, dtype=jnp.int32)
    direction = (index // freqs).astype(jnp.float32)
    level = (index % freqs).astype(jnp.float32)
    theta = 2.0 * jnp.pi * (direction + 0.5) / (components // freqs)
    speed = jnp.power(jnp.float32(1.1), -level)
    return (
        (0.45 * speed * jnp.cos(theta))[:, None, None],
        (0.45 * speed * jnp.sin(theta))[:, None, None],
    )


def lat_sides(centre):
    below = passed_along(centre[:, :, -1:], "lat", 1)
    above = passed_along(centre[:, :, :1], "lat", -1)
    return (below, above)


def advect(lon_wide, below, above, east, north):
    centre = lon_wide[:, 1:-1, :]
    south_side = jnp.concatenate([below, centre[:, :, :-1]], axis=2)
    north_side = jnp.concatenate([centre[:, :, 1:], above], axis=2)
    result = (1.0 - jnp.abs(east) - jnp.abs(north)) * centre
    result = (
        result
        + jnp.maximum(east, 0.0) * lon_wide[:, :-2, :]
        + jnp.maximum(-east, 0.0) * lon_wide[:, 2:, :]
    )
    result = result + jnp.maximum(north, 0.0) * south_side + jnp.maximum(-north, 0.0) * north_side
    return result


def source(advected, transfer, maskf):
    flat = advected.reshape(advected.shape[0], -1).astype(jnp.bfloat16)
    added = jnp.dot(transfer, flat, preferred_element_type=jnp.float32).reshape(advected.shape)
    return maskf * (advected + 0.5 * added)


def ocean_update(padded, ocean_u, ocean_v, drift_u, drift_v, maskf, coriolis):
    levels = ocean_u.shape[0]

    def dxx(q):
        return 0.5 * (q[2:, 1:-1] - q[:-2, 1:-1])

    def dyy(q):
        return 0.5 * (q[1:-1, 2:] - q[1:-1, :-2])

    sxx = padded[2 * levels]
    sxy = padded[2 * levels + 1]
    syy = padded[2 * levels + 2]
    force_x = -(dxx(sxx) + dyy(sxy))
    force_y = -(dxx(sxy) + dyy(syy))

    def laplace(q):
        return (
            q[:, 2:, 1:-1]
            + q[:, :-2, 1:-1]
            + q[:, 1:-1, 2:]
            + q[:, 1:-1, :-2]
            - 4.0 * q[:, 1:-1, 1:-1]
        )

    decay = jnp.exp(-jnp.arange(levels, dtype=jnp.float32) / 3.0)[:, None, None]
    lap_u = laplace(padded[:levels])
    lap_v = laplace(padded[levels : 2 * levels])
    fcor = coriolis[None, None, :]
    new_u = maskf * (
        ocean_u + 0.5 * fcor * (ocean_v + decay * drift_v) + 0.5 * decay * force_x + 0.1 * lap_u
    )
    new_v = maskf * (
        ocean_v - 0.5 * fcor * (ocean_u + decay * drift_u) + 0.5 * decay * force_y + 0.1 * lap_v
    )
    return (new_u, new_v)


def local(
    spectrum,
    sea_mask,
    transfer,
    bulk_weight,
    remap_cell,
    remap_weight,
    ocean_u,
    ocean_v,
    ocean_mask,
    coriolis,
):
    components, width_x, width_y = spectrum.shape
    east, north = courant(components, NFREQ)
    maskf = sea_mask.astype(jnp.float32)[None]
    state = spectrum * maskf
    for step in range(2):
        extended = with_halo(state, (("lon", 1),), 1, True)
        below, above = lat_sides(state)
        state = source(advect(extended, below, above, east, north), transfer, maskf)
    flat = state.reshape(components, -1)
    bulk = jnp.dot(
        bulk_weight, flat, precision=lax.Precision.HIGHEST, preferred_element_type=jnp.float32
    )
    bulk = bulk.reshape(5, width_x, width_y)
    near = with_halo(bulk, (("lon", 1),), width_x, True).reshape(5, -1)
    lat_index = lax.axis_index("lat")
    total_y = width_y * lax.axis_size("lat")
    ocean_rows = jnp.arange(remap_cell.shape[0], dtype=jnp.int32)[:, None, None]
    local_lon = ocean_rows // 3 + remap_cell // total_y
    local_lat = remap_cell % total_y - lat_index * width_y
    position = local_lon * width_y + local_lat
    taken = jnp.take(near, position.reshape(-1), axis=1).reshape((5,) + remap_cell.shape)
    forcing = jnp.sum(taken * remap_weight[None], axis=-1)
    stacked = jnp.concatenate([ocean_u, ocean_v, forcing[:3]], axis=0)
    padded = with_halo(stacked, (("lon", 1),), 1, True)
    padded = with_halo(padded, (("lat", 2),), 1, False)
    new_u, new_v = ocean_update(
        padded,
        ocean_u,
        ocean_v,
        forcing[3],
        forcing[4],
        ocean_mask.astype(jnp.float32)[None],
        coriolis,
    )
    return (state, new_u, new_v)


def solution(mesh):
    placed = (
        P(None, "lon", "lat"),
        P("lon", "lat"),
        P(),
        P(),
        P("lon", "lat", None),
        P("lon", "lat", None),
        P(None, "lon", "lat"),
        P(None, "lon", "lat"),
        P("lon", "lat"),
        P("lat"),
    )
    return jax.shard_map(
        local,
        mesh=mesh,
        in_specs=placed,
        out_specs=(P(None, "lon", "lat"), P(None, "lon", "lat"), P(None, "lon", "lat")),
        check_vma=False,
    )
```

profile of v0, /device:TPU:1, one launch (start us, length us, event | category | flops | bytes accessed | tf_op | source)
XLA Modules:
  0.0 379.4 jit_solution(12197901482529716272)
XLA Ops:
  4.9 5.7 %fusion.69 = (f32[1296,8,1]{2,0,1:T(8,128)}, f32[1296,8,1]{2,0,1:T(8,128)}) fusion(f32[1296,8,128]{2,0,1:T(8,128)S(1)} %copy_multiply_fusion), kind=kLoop, calls=%fused_computation.152 | loop fusion | bytes 165888 | tf_op jit(solution)/shard_map/slice | solution.py:41
  10.6 4.1 %copy.38 = f32[1296,8,1]{0,1,2:T(8,128)S(1)} copy(f32[1296,8,1]{2,0,1:T(8,128)} %get-tuple-element.25) | data formatting | bytes 82944 | tf_op jit(solution)/shard_map/slice | solution.py:41
  14.7 4.6 %collective-permute-start.2 = (f32[1296,8,1]{0,1,2:T(8,128)S(1)}, f32[1296,8,1]{0,1,2:T(8,128)S(1)}, u32[]{:S(2)}, u32[]{:S(2)}) collective-permute-start(f32[1296,8,1]{0,1,2:T(8,128)S(1)} %copy.38), channel_id=1, source_target_pairs={{0,1},{1,2},{2,3},{4,5},{5,6},{6,7},{8,9},{9,10},{10,11},{12,13},{... | collective-permute-start | bytes 124424 | tf_op jit(solution)/shard_map/ppermute | solution.py:12
  19.4 4.1 %copy.40 = f32[1296,8,1]{0,1,2:T(8,128)S(1)} copy(f32[1296,8,1]{2,0,1:T(8,128)} %get-tuple-element.26) | data formatting | bytes 82944 | tf_op jit(solution)/shard_map/slice | solution.py:42
  29.3 6.5 %collective-permute-start.1 = (f32[1296,1,128]{2,0,1:T(8,128)S(1)}, f32[1296,1,128]{2,0,1:T(8,128)S(1)}, u32[]{:S(2)}, u32[]{:S(2)}) collective-permute-start(f32[1296,1,128]{2,0,1:T(8,128)S(1)} %get-tuple-element.24), channel_id=1, source_target_pairs={{4,0},{8,4},{12,8},{16,12},{20,16},{24,20},{28,24},{32,28},{36,32}... | collective-permute-start | bytes 1990664 | tf_op jit(solution)/shard_map/ppermute | solution.py:23
  39.2 6.7 %reshape.167 = s32[36864,1]{0,1:T(1,128)S(1)} reshape(s32[24,384,4]{2,1,0:T(8,128)} %copy.53) | data formatting | bytes 294912 | tf_op jit(solution)/shard_map/reshape | solution.py:135
  46.1 9.5 %fusion.70 = (f32[1296,8,127]{2,0,1:T(8,128)}, f32[1296,8,127]{2,0,1:T(8,128)}) fusion(f32[1296,8,128]{2,0,1:T(8,128)} %copy-done.1), kind=kLoop, calls=%fused_computation.153 | loop fusion | bytes 21067776 | tf_op jit(solution)/shard_map/slice | solution.py:48
  63.3 13.4 %convert_bitcast_fusion.1 = (bf16[8,162,8,128]{3,2,1,0:T(8,128)(2,1)S(1)}, f32[1296,8,128]{2,0,1:T(8,128)S(1)}) fusion(f32[1296,8,1]{2,0,1:T(8,128)} %copy.41, f32[1296,8,127]{2,0,1:T(8,128)} %get-tuple-element.28, f32[1296]{0:T(1024)S(1)} %get-tuple-element.37, f32[1296,8,127]{2,0,1:T(8,128)} %get-tuple-element.27, f32[1296,8,1]{2,0,1:T(8,128)} %copy.39, ...), kind=kLoop, calls=%fused_computation.39 | loop fusion | flops 18579456 | bytes 25240896
  76.7 4.3 %multiply_bitcast_fusion.1 = f32[162,8,8,128]{3,2,1,0:T(8,128)S(1)} fusion(bf16[1296,1296]{1,0:T(8,128)(2,1)S(1)} %copy-done.10, bf16[8,162,8,128]{3,2,1,0:T(8,128)(2,1)S(1)} %get-tuple-element.15), kind=kOutput, calls=%fused_computation.31 | convolution fusion | flops 3441180672 | bytes 11321856 | tf_op jit(solution)/shard_map/dot_general | solution.py:62
  81.8 5.7 %fusion.66 = (f32[1296,8,1]{2,0,1:T(8,128)}, f32[1296,8,1]{2,0,1:T(8,128)}) fusion(f32[1296,8,128]{2,0,1:T(8,128)S(1)} %fusion.4), kind=kLoop, calls=%fused_computation.149 | loop fusion | bytes 165888 | tf_op jit(solution)/shard_map/slice | solution.py:41
  87.6 4.1 %copy.44 = f32[1296,8,1]{0,1,2:T(8,128)S(1)} copy(f32[1296,8,1]{2,0,1:T(8,128)} %get-tuple-element.19) | data formatting | bytes 82944 | tf_op jit(solution)/shard_map/slice | solution.py:41
  95.1 4.1 %copy.46 = f32[1296,8,1]{0,1,2:T(8,128)S(1)} copy(f32[1296,8,1]{2,0,1:T(8,128)} %get-tuple-element.20) | data formatting | bytes 82944 | tf_op jit(solution)/shard_map/slice | solution.py:42
  101.2 7.2 %collective-permute-start.5 = (f32[1296,1,128]{2,0,1:T(8,128)S(1)}, f32[1296,1,128]{2,0,1:T(8,128)S(1)}, u32[]{:S(2)}, u32[]{:S(2)}) collective-permute-start(f32[1296,1,128]{2,0,1:T(8,128)S(1)} %get-tuple-element.18), channel_id=1, source_target_pairs={{4,0},{8,4},{12,8},{16,12},{20,16},{24,20},{28,24},{32,28},{36,32}... | collective-permute-start | bytes 1990664 | tf_op jit(solution)/shard_map/ppermute | solution.py:23
  108.4 9.5 %fusion.67 = (f32[1296,8,127]{2,0,1:T(8,128)}, f32[1296,8,127]{2,0,1:T(8,128)}) fusion(f32[1296,8,128]{2,0,1:T(8,128)} %copy-done.2), kind=kLoop, calls=%fused_computation.150 | loop fusion | bytes 21067776 | tf_op jit(solution)/shard_map/slice | solution.py:48
  125.6 4.1 %collective-permute-done.5 = f32[1296,1,128]{2,0,1:T(8,128)S(1)} collective-permute-done((f32[1296,1,128]{2,0,1:T(8,128)S(1)}, f32[1296,1,128]{2,0,1:T(8,128)S(1)}, u32[]{:S(2)}, u32[]{:S(2)}) %collective-permute-start.5) | collective-permute-done | bytes 663584 | tf_op jit(solution)/shard_map/ppermute | solution.py:23
  129.6 13.2 %convert_bitcast_fusion = (bf16[8,162,8,128]{3,2,1,0:T(8,128)(2,1)S(1)}, f32[1296,8,128]{2,0,1:T(8,128)S(1)}) fusion(f32[1296,8,1]{2,0,1:T(8,128)} %copy.47, f32[1296,8,127]{2,0,1:T(8,128)} %get-tuple-element.22, f32[1296]{0:T(1024)S(1)} %get-tuple-element.37, f32[1296,8,127]{2,0,1:T(8,128)} %get-tuple-element.21, f32[1296,8,1]{2,0,1:T(8,128)} %copy.45, ...), kind=kLoop, calls=%fused_computation.38 | loop fusion | flops 18579456 | bytes 25240896
  142.8 4.3 %multiply_bitcast_fusion = f32[162,8,8,128]{3,2,1,0:T(8,128)S(1)} fusion(bf16[1296,1296]{1,0:T(8,128)(2,1)S(1)} %copy-done.11, bf16[8,162,8,128]{3,2,1,0:T(8,128)(2,1)S(1)} %get-tuple-element.13), kind=kOutput, calls=%fused_computation.30 | convolution fusion | flops 3441180672 | bytes 11321856 | tf_op jit(solution)/shard_map/dot_general | solution.py:62
  155.7 4.4 %collective-permute-start.9 = (f32[5,8,128]{2,1,0:T(8,128)S(1)}, f32[5,8,128]{2,1,0:T(8,128)S(1)}, u32[]{:S(2)}, u32[]{:S(2)}) collective-permute-start(f32[5,8,128]{2,1,0:T(8,128)S(1)} %bitcast.61), channel_id=1, source_target_pairs={{4,0},{8,4},{12,8},{16,12},{20,16},{24,20},{28,24},{32,28},{36,32}... | collective-permute-start | bytes 61448 | tf_op jit(solution)/shard_map/ppermute | solution.py:23
  165.8 122.5 %gather_fusion = f32[36864,5]{1,0:T(8,128)} fusion(f32[5,3072]{0,1:T(8,128)S(1)} %bitcast.54, s32[36864]{0:T(1024)S(1)} %broadcast_clamp_fusion), kind=kCustom, calls=%fused_computation | custom fusion | bytes 1622016 | tf_op jit(solution)/shard_map/jit(_take)/gather | solution.py:135
  288.3 55.7 %multiply_reduce_fusion = f32[5,24,384]{0,2,1:T(8,128)} fusion(f32[5,24,384,4]{0,3,2,1:T(4,128)} %bitcast.58, f32[24,384,4]{2,1,0:T(8,128)} %copy.54, pred[24,384,4]{2,1,0:T(8,128)(4,1)S(1)} %copy.50), kind=kLoop, calls=%fused_computation.1 | loop fusion | flops 506880 | bytes 1105920 | tf_op jit(solution)/shard_map/reduce_sum | solution.py:136
  347.9 7.2 %collective-permute-start.11 = (f32[19,1,384]{2,1,0:T(1,128)S(1)}, f32[19,1,384]{2,1,0:T(1,128)S(1)}, u32[]{:S(2)}, u32[]{:S(2)}) collective-permute-start(f32[19,1,384]{2,1,0:T(1,128)S(1)} %get-tuple-element.34), channel_id=1, source_target_pairs={{4,0},{8,4},{12,8},{16,12},{20,16},{24,20},{28,24},{32,28},{36,32}... | collective-permute-start | bytes 87560 | tf_op jit(solution)/shard_map/ppermute | solution.py:23
  355.1 7.5 %copy.56 = f32[1296,8,128]{2,1,0:T(8,128)} copy(f32[1296,8,128]{2,0,1:T(8,128)} %copy-done.3) | data formatting | bytes 10616832
  362.8 5.5 %collective-permute-start.12 = (f32[19,26,1]{2,1,0:T(8,128)S(1)}, f32[19,26,1]{2,1,0:T(8,128)S(1)}, u32[]{:S(2)}, u32[]{:S(2)}) collective-permute-start(f32[19,26,1]{2,1,0:T(8,128)S(1)} %get-tuple-element.32), channel_id=1, source_target_pairs={{0,1},{1,2},{2,3},{4,5},{5,6},{6,7},{8,9},{9,10},{10,11},{12,13},{... | collective-permute-start | bytes 5936 | tf_op jit(solution)/shard_map/ppermute | solution.py:22
  370.3 4.9 %slice_reduce_fusion = (f32[24,384]{1,0:T(8,128)S(1)}, f32[24,384]{1,0:T(8,128)S(1)}) fusion(f32[5,24,384]{0,2,1:T(8,128)S(1)} %bitcast.57), kind=kLoop, calls=%fused_computation.32 | loop fusion | bytes 147456 | tf_op jit(solution)/shard_map/slice | solution.py:144
  (85 shorter events, 59.2 us)
Async XLA Ops:
  0.6 149.4 %copy-start = (f32[5,1296]{1,0:T(8,128)S(1)}, f32[5,1296]{1,0:T(8,128)}, u32[]{:S(2)}) copy-start(f32[5,1296]{1,0:T(8,128)} %param.13) | copy-start | bytes 77764
  14.7 21.1 %copy-start.7 = (s32[24,384,4]{1,2,0:T(4,128)S(1)}, s32[24,384,4]{1,2,0:T(4,128)}, u32[]{:S(2)}) copy-start(s32[24,384,4]{1,2,0:T(4,128)} %param.14) | copy-start | bytes 442372
  14.7 41.1 %collective-permute-start.2 = (f32[1296,8,1]{0,1,2:T(8,128)S(1)}, f32[1296,8,1]{0,1,2:T(8,128)S(1)}, u32[]{:S(2)}, u32[]{:S(2)}) collective-permute-start(f32[1296,8,1]{0,1,2:T(8,128)S(1)} %copy.38), channel_id=1, source_target_pairs={{0,1},{1,2},{2,3},{4,5},{5,6},{6,7},{8,9},{9,10},{10,11},{12,13},{... | collective-permute-start | bytes 124424 | tf_op jit(solution)/shard_map/ppermute | solution.py:12
  23.5 36.1 %collective-permute-start.3 = (f32[1296,8,1]{0,1,2:T(8,128)S(1)}, f32[1296,8,1]{0,1,2:T(8,128)S(1)}, u32[]{:S(2)}, u32[]{:S(2)}) collective-permute-start(f32[1296,8,1]{0,1,2:T(8,128)S(1)} %copy.40), channel_id=1, source_target_pairs={{1,0},{2,1},{3,2},{5,4},{6,5},{7,6},{9,8},{10,9},{11,10},{13,12},{... | collective-permute-start | bytes 124424 | tf_op jit(solution)/shard_map/ppermute | solution.py:12
  26.8 36.5 %collective-permute-start = (f32[1296,1,128]{2,0,1:T(8,128)S(1)}, f32[1296,1,128]{2,0,1:T(8,128)S(1)}, u32[]{:S(2)}, u32[]{:S(2)}) collective-permute-start(f32[1296,1,128]{2,0,1:T(8,128)S(1)} %get-tuple-element.23), channel_id=1, source_target_pairs={{0,4},{4,8},{8,12},{12,16},{16,20},{20,24},{24,28},{28,32},{32,36}... | collective-permute-start | bytes 1990664 | tf_op jit(solution)/shard_map/ppermute | solution.py:22
  29.3 34.0 %collective-permute-start.1 = (f32[1296,1,128]{2,0,1:T(8,128)S(1)}, f32[1296,1,128]{2,0,1:T(8,128)S(1)}, u32[]{:S(2)}, u32[]{:S(2)}) collective-permute-start(f32[1296,1,128]{2,0,1:T(8,128)S(1)} %get-tuple-element.24), channel_id=1, source_target_pairs={{4,0},{8,4},{12,8},{16,12},{20,16},{24,20},{28,24},{32,28},{36,32}... | collective-permute-start | bytes 1990664 | tf_op jit(solution)/shard_map/ppermute | solution.py:23
  63.3 13.4 %copy-start.10 = (bf16[1296,1296]{1,0:T(8,128)(2,1)S(1)}, bf16[1296,1296]{1,0:T(8,128)(2,1)}, u32[]{:S(2)}) copy-start(bf16[1296,1296]{1,0:T(8,128)(2,1)} %param.12) | copy-start | bytes 10077700
  91.7 26.2 %collective-permute-start.6 = (f32[1296,8,1]{0,1,2:T(8,128)S(1)}, f32[1296,8,1]{0,1,2:T(8,128)S(1)}, u32[]{:S(2)}, u32[]{:S(2)}) collective-permute-start(f32[1296,8,1]{0,1,2:T(8,128)S(1)} %copy.44), channel_id=1, source_target_pairs={{0,1},{1,2},{2,3},{4,5},{5,6},{6,7},{8,9},{9,10},{10,11},{12,13},{... | collective-permute-start | bytes 124424 | tf_op jit(solution)/shard_map/ppermute | solution.py:12
  99.2 22.7 %collective-permute-start.7 = (f32[1296,8,1]{0,1,2:T(8,128)S(1)}, f32[1296,8,1]{0,1,2:T(8,128)S(1)}, u32[]{:S(2)}, u32[]{:S(2)}) collective-permute-start(f32[1296,8,1]{0,1,2:T(8,128)S(1)} %copy.46), channel_id=1, source_target_pairs={{1,0},{2,1},{3,2},{5,4},{6,5},{7,6},{9,8},{10,9},{11,10},{13,12},{... | collective-permute-start | bytes 124424 | tf_op jit(solution)/shard_map/ppermute | solution.py:12
  101.1 24.5 %collective-permute-start.4 = (f32[1296,1,128]{2,0,1:T(8,128)S(1)}, f32[1296,1,128]{2,0,1:T(8,128)S(1)}, u32[]{:S(2)}, u32[]{:S(2)}) collective-permute-start(f32[1296,1,128]{2,0,1:T(8,128)S(1)} %get-tuple-element.17), channel_id=1, source_target_pairs={{0,4},{4,8},{8,12},{12,16},{16,20},{20,24},{24,28},{28,32},{32,36}... | collective-permute-start | bytes 1990664 | tf_op jit(solution)/shard_map/ppermute | solution.py:22
  101.2 28.4 %collective-permute-start.5 = (f32[1296,1,128]{2,0,1:T(8,128)S(1)}, f32[1296,1,128]{2,0,1:T(8,128)S(1)}, u32[]{:S(2)}, u32[]{:S(2)}) collective-permute-start(f32[1296,1,128]{2,0,1:T(8,128)S(1)} %get-tuple-element.18), channel_id=1, source_target_pairs={{4,0},{8,4},{12,8},{16,12},{20,16},{24,20},{28,24},{32,28},{36,32}... | collective-permute-start | bytes 1990664 | tf_op jit(solution)/shard_map/ppermute | solution.py:23
  129.6 13.2 %copy-start.11 = (bf16[1296,1296]{1,0:T(8,128)(2,1)S(1)}, bf16[1296,1296]{1,0:T(8,128)(2,1)}, u32[]{:S(2)}) copy-start(bf16[1296,1296]{1,0:T(8,128)(2,1)} %param.12) | copy-start | bytes 10077700
  150.0 12.3 %copy-start.6 = (f32[24,384,4]{1,2,0:T(4,128)S(1)}, f32[24,384,4]{1,2,0:T(4,128)}, u32[]{:S(2)}) copy-start(f32[24,384,4]{1,2,0:T(4,128)} %param.15) | copy-start | bytes 442372
  152.9 12.4 %collective-permute-start.8 = (f32[5,8,128]{2,1,0:T(8,128)S(1)}, f32[5,8,128]{2,1,0:T(8,128)S(1)}, u32[]{:S(2)}, u32[]{:S(2)}) collective-permute-start(f32[5,8,128]{2,1,0:T(8,128)S(1)} %bitcast.60), channel_id=1, source_target_pairs={{0,4},{4,8},{8,12},{12,16},{16,20},{20,24},{24,28},{28,32},{32,36}... | collective-permute-start | bytes 61448 | tf_op jit(solution)/shard_map/ppermute | solution.py:22
  155.7 9.6 %collective-permute-start.9 = (f32[5,8,128]{2,1,0:T(8,128)S(1)}, f32[5,8,128]{2,1,0:T(8,128)S(1)}, u32[]{:S(2)}, u32[]{:S(2)}) collective-permute-start(f32[5,8,128]{2,1,0:T(8,128)S(1)} %bitcast.61), channel_id=1, source_target_pairs={{4,0},{8,4},{12,8},{16,12},{20,16},{24,20},{28,24},{32,28},{36,32}... | collective-permute-start | bytes 61448 | tf_op jit(solution)/shard_map/ppermute | solution.py:23
  288.3 59.4 %copy-start.4 = (f32[8,24,384]{2,1,0:T(8,128)S(1)}, f32[8,24,384]{2,1,0:T(8,128)}, u32[]{:S(2)}) copy-start(f32[8,24,384]{2,1,0:T(8,128)} %param.17) | copy-start | bytes 884740
  288.3 59.5 %copy-start.5 = (f32[8,24,384]{2,1,0:T(8,128)S(1)}, f32[8,24,384]{2,1,0:T(8,128)}, u32[]{:S(2)}) copy-start(f32[8,24,384]{2,1,0:T(8,128)} %param.16) | copy-start | bytes 884740
  343.9 11.1 %copy-start.8 = (s32[24,384]{1,0:T(8,128)S(1)}, s32[24,384]{1,0:T(8,128)}, u32[]{:S(2)}) copy-start(s32[24,384]{1,0:T(8,128)} %param.18) | copy-start | bytes 110596
  347.8 14.8 %collective-permute-start.10 = (f32[19,1,384]{2,1,0:T(1,128)S(1)}, f32[19,1,384]{2,1,0:T(1,128)S(1)}, u32[]{:S(2)}, u32[]{:S(2)}) collective-permute-start(f32[19,1,384]{2,1,0:T(1,128)S(1)} %get-tuple-element.33), channel_id=1, source_target_pairs={{0,4},{4,8},{8,12},{12,16},{16,20},{20,24},{24,28},{28,32},{32,36}... | collective-permute-start | bytes 87560 | tf_op jit(solution)/shard_map/ppermute | solution.py:22
  347.9 14.8 %collective-permute-start.11 = (f32[19,1,384]{2,1,0:T(1,128)S(1)}, f32[19,1,384]{2,1,0:T(1,128)S(1)}, u32[]{:S(2)}, u32[]{:S(2)}) collective-permute-start(f32[19,1,384]{2,1,0:T(1,128)S(1)} %get-tuple-element.34), channel_id=1, source_target_pairs={{4,0},{8,4},{12,8},{16,12},{20,16},{24,20},{28,24},{32,28},{36,32}... | collective-permute-start | bytes 87560 | tf_op jit(solution)/shard_map/ppermute | solution.py:23
  355.1 15.2 %slice-start = ((s8[4718592]{0:T(1024)(128)(4,1)}), s8[4194304]{0:T(1024)(128)(4,1)S(1)}, s32[]{:S(2)}) async-start(s8[4718592]{0:T(1024)(128)(4,1)} %bitcast.56), calls=%async_computation | async-start | bytes 8388608
  355.1 15.2 %slice-start.1 = ((s8[4718592]{0:T(1024)(128)(4,1)}), s8[524288]{0:T(1024)(128)(4,1)S(1)}, s32[]{:S(2)}) async-start(s8[4718592]{0:T(1024)(128)(4,1)} %bitcast.56), calls=%async_computation.1 | async-start | bytes 1048576
  362.8 12.4 %collective-permute-start.12 = (f32[19,26,1]{2,1,0:T(8,128)S(1)}, f32[19,26,1]{2,1,0:T(8,128)S(1)}, u32[]{:S(2)}, u32[]{:S(2)}) collective-permute-start(f32[19,26,1]{2,1,0:T(8,128)S(1)} %get-tuple-element.32), channel_id=1, source_target_pairs={{0,1},{1,2},{2,3},{4,5},{5,6},{6,7},{8,9},{9,10},{10,11},{12,13},{... | collective-permute-start | bytes 5936 | tf_op jit(solution)/shard_map/ppermute | solution.py:22
  368.3 8.2 %collective-permute-start.13 = (f32[19,26,1]{2,1,0:T(8,128)S(1)}, f32[19,26,1]{2,1,0:T(8,128)S(1)}, u32[]{:S(2)}, u32[]{:S(2)}) collective-permute-start(f32[19,26,1]{2,1,0:T(8,128)S(1)} %get-tuple-element.31), channel_id=1, source_target_pairs={{1,0},{2,1},{3,2},{5,4},{6,5},{7,6},{9,8},{10,9},{11,10},{13,12},{... | collective-permute-start | bytes 5936 | tf_op jit(solution)/shard_map/ppermute | solution.py:23
  (4 other events, 23.9 us)
where the time goes:
time: 384 us; the launch traced here: 379 us
  local copies, waits for them, and re-layouts  220 us (57%)
  other arithmetic  91.3 us (24%)
  starting transfers between devices  50 us (13%)
  matrix products  11.5 us (3%)
  waiting for transfers between devices  5.38 us (1%)
    gather x1, local copies, waits for them, and re-layouts, local(): jnp.take(near, position.reshape(-1), axis=1)  122 us
    reduce_sum x1, other arithmetic, local(): forcing = jnp.sum(taken * remap_weight[None], axis=-1)  55.7 us
    ppermute x5, starting transfers between devices, with_halo(): after = lax.ppermute(first, axis, down)  27.3 us
    unnamed x3, other arithmetic  26.5 us
    slice x4, local copies, waits for them, and re-layouts, lat_sides(): below = passed_along(centre[:, :, -1:], 'lat', 1)  19.7 us
    slice x2, local copies, waits for them, and re-layouts, advect(): south_side = jnp.concatenate([below, centre[:, :, :-1]], axis=2)  19 us
    ppermute x4, local copies, waits for them, and re-layouts, passed_along(): lax.ppermute(value, axis, [(source, source + steps) for source in range(f...  15.2 us
    unnamed x31, local copies, waits for them, and re-layouts  12.8 us
  transfers between devices with their start and end apart: 14, of which 2 were waited for; matrix products, arithmetic and copies ran while one was open for 19% of the time, Pallas kernels for 0%

commit v1 on v0

--- a/solution.py
+++ b/solution.py
@@ -1,6 +1,8 @@
 import jax
 import jax.numpy as jnp
 from jax import lax
+from jax.experimental import pallas as pl
+from jax.experimental.pallas import tpu as pltpu
 from jax.sharding import PartitionSpec as P
 
 NFREQ = 36
@@ -98,6 +100,57 @@
         ocean_v - 0.5 * fcor * (ocean_u + decay * drift_u) + 0.5 * decay * force_y + 0.1 * lap_v
     )
     return (new_u, new_v)
+
+
+def remap_kernel(near_ref, cell_ref, weight_ref, out_ref, near3, cells, weights):
+    quantities, columns, lanes = near_ref.shape
+    rows, taps, width = cell_ref.shape
+    for i in range(columns):
+        for q in range(quantities):
+            near3[q, pl.ds(3 * i, 3), :] = jnp.broadcast_to(near_ref[q, pl.ds(i, 1), :], (3, lanes))
+    for i in range(rows):
+        for t in range(taps):
+            cells[t, pl.ds(i, 1), :] = cell_ref[i, pl.ds(t, 1), :]
+            weights[t, pl.ds(i, 1), :] = weight_ref[i, pl.ds(t, 1), :]
+
+    def block(jb, carry):
+        lane = pl.multiple_of(jb * lanes, lanes)
+        for i0 in range(0, rows, 8):
+            codes = [cells[t, pl.ds(i0, 8), pl.ds(lane, lanes)] for t in range(taps)]
+            places = [c & (lanes - 1) for c in codes]
+            offsets = [c >> 9 for c in codes]
+            taken = [[jnp.zeros((8, lanes), jnp.float32)] * quantities for t in range(taps)]
+            for o in range(17):
+                hits = [offset == o for offset in offsets]
+                for q in range(quantities):
+                    source = near3[q, pl.ds(i0 + 3 * o, 8), :]
+                    for t in range(taps):
+                        got = jnp.take_along_axis(source, places[t], axis=1, mode="promise_in_bounds")
+                        taken[t][q] = jnp.where(hits[t], got, taken[t][q])
+            for q in range(quantities):
+                total = 0.0
+                for t in range(taps):
+                    total = total + taken[t][q] * weights[t, pl.ds(i0, 8), pl.ds(lane, lanes)]
+                out_ref[q, pl.ds(i0, 8), pl.ds(lane, lanes)] = total
+        return carry
+
+    lax.fori_loop(0, width // lanes, block, 0)
+
+
+def remapped(near, cell, weight):
+    quantities, columns, lanes = near.shape
+    rows, taps, width = cell.shape
+    return pl.pallas_call(
+        remap_kernel,
+        out_shape=jax.ShapeDtypeStruct((quantities, rows, width), jnp.float32),
+        in_specs=[pl.BlockSpec(memory_space=pltpu.VMEM)] * 3,
+        out_specs=pl.BlockSpec(memory_space=pltpu.VMEM),
+        scratch_shapes=[
+            pltpu.VMEM((quantities, 3 * columns, lanes), jnp.float32),
+            pltpu.VMEM((taps, rows, width), jnp.int32),
+            pltpu.VMEM((taps, rows, width), jnp.float32),
+        ],
+    )(near, cell, weight)
 
 
 def local(
@@ -125,15 +178,10 @@
         bulk_weight, flat, precision=lax.Precision.HIGHEST, preferred_element_type=jnp.float32
     )
     bulk = bulk.reshape(5, width_x, width_y)
-    near = with_halo(bulk, (("lon", 1),), width_x, True).reshape(5, -1)
-    lat_index = lax.axis_index("lat")
-    total_y = width_y * lax.axis_size("lat")
-    ocean_rows = jnp.arange(remap_cell.shape[0], dtype=jnp.int32)[:, None, None]
-    local_lon = ocean_rows // 3 + remap_cell // total_y
-    local_lat = remap_cell % total_y - lat_index * width_y
-    position = local_lon * width_y + local_lat
-    taken = jnp.take(near, position.reshape(-1), axis=1).reshape((5,) + remap_cell.shape)
-    forcing = jnp.sum(taken * remap_weight[None], axis=-1)
+    near = with_halo(bulk, (("lon", 1),), width_x, True)
+    forcing = remapped(
+        near, jnp.transpose(remap_cell, (0, 2, 1)), jnp.transpose(remap_weight, (0, 2, 1))
+    )
     stacked = jnp.concatenate([ocean_u, ocean_v, forcing[:3]], axis=0)
     padded = with_halo(stacked, (("lon", 1),), 1, True)
     padded = with_halo(padded, (("lat", 2),), 1, False)

time: 384 us -> 206 us (0.54)
  local copies, waits for them, and re-layouts: 220 us -> 74.7 us
  other arithmetic: 91.3 us -> 35.4 us
  waiting for transfers between devices: 5.38 us -> 20.9 us
  Pallas kernels: 0 us -> 10.7 us
    gather x1 -> x0, local copies, waits for them, and re-layouts: 122 us -> none  [local(): jnp.take(near, position.reshape(-1), axis=1)]
    reduce_sum x1 -> x0, other arithmetic: 55.7 us -> none  [local(): forcing = jnp.sum(taken * remap_weight[None], axis=-1)]
    ppermute x5, waiting for transfers between devices: 5.36 us -> 18.6 us  [with_halo(): after = lax.ppermute(first, axis, down)]
    pallas_call x0 -> x1, Pallas kernels: none -> 10.7 us  [remapped(): pl.pallas_call(remap_kernel, out_shape=jax.ShapeDtypeStruct((quantities,...]
    reshape x1 -> x0, local copies, waits for them, and re-layouts: 6.72 us -> none  [local(): position.reshape(-1)]
    slice x1 -> x0, local copies, waits for them, and re-layouts: 4.95 us -> none  [local(): forcing[3]]
    unnamed x31 -> x22, local copies, waits for them, and re-layouts: 12.8 us -> 9.76 us
    unnamed x3 -> x2, other arithmetic: 26.5 us -> 26.2 us
  transfers between devices with their start and end apart: 14 -> 14, of which waited for: 2 -> 5; matrix products, arithmetic and copies ran while one was open for 19% -> 25% of each run, Pallas kernels for 0% -> 0%
where the time goes in v1:
time: 206 us; the launch traced here: 205 us
  local copies, waits for them, and re-layouts  74.7 us (36%)
  starting transfers between devices  50.9 us (25%)
  other arithmetic  35.4 us (17%)
  waiting for transfers between devices  20.9 us (10%)
  matrix products  11.5 us (6%)
  Pallas kernels  10.7 us (5%)
    unnamed x2, other arithmetic  26.2 us
    ppermute x5, starting transfers between devices, with_halo(): after = lax.ppermute(first, axis, down)  23.9 us
    slice x4, local copies, waits for them, and re-layouts, lat_sides(): below = passed_along(centre[:, :, -1:], 'lat', 1)  19.6 us
    slice x2, local copies, waits for them, and re-layouts, advect(): south_side = jnp.concatenate([below, centre[:, :, :-1]], axis=2)  19 us
    ppermute x5, waiting for transfers between devices, with_halo(): after = lax.ppermute(first, axis, down)  18.6 us
    ppermute x4, local copies, waits for them, and re-layouts, passed_along(): lax.ppermute(value, axis, [(source, source + steps) for source in range(f...  14.9 us
    ppermute x5, starting transfers between devices, with_halo(): before = lax.ppermute(last, axis, up)  14.7 us
    ppermute x4, starting transfers between devices, passed_along(): lax.ppermute(value, axis, [(source, source + steps) for source in range(f...  12.4 us
  transfers between devices with their start and end apart: 14, of which 5 were waited for; matrix products, arithmetic and copies ran while one was open for 25% of the time, Pallas kernels for 0%

profile of v1, /device:TPU:1, one launch (start us, length us, event | category | flops | bytes accessed | tf_op | source)
XLA Modules:
  0.0 205.1 jit_solution(9540552138521824214)
XLA Ops:
  4.9 5.7 %fusion.62 = (f32[1296,8,1]{2,0,1:T(8,128)}, f32[1296,8,1]{2,0,1:T(8,128)}) fusion(f32[1296,8,128]{2,0,1:T(8,128)S(1)} %copy_multiply_fusion), kind=kLoop, calls=%fused_computation.130 | loop fusion | bytes 165888 | tf_op jit(solution)/shard_map/slice | solution.py:43
  10.6 4.1 %copy.26 = f32[1296,8,1]{0,1,2:T(8,128)S(1)} copy(f32[1296,8,1]{2,0,1:T(8,128)} %get-tuple-element.21) | data formatting | bytes 82944 | tf_op jit(solution)/shard_map/slice | solution.py:43
  14.7 4.5 %collective-permute-start.2 = (f32[1296,8,1]{0,1,2:T(8,128)S(1)}, f32[1296,8,1]{0,1,2:T(8,128)S(1)}, u32[]{:S(2)}, u32[]{:S(2)}) collective-permute-start(f32[1296,8,1]{0,1,2:T(8,128)S(1)} %copy.26), channel_id=1, source_target_pairs={{0,1},{1,2},{2,3},{4,5},{5,6},{6,7},{8,9},{9,10},{10,11},{12,13},{... | collective-permute-start | bytes 124424 | tf_op jit(solution)/shard_map/ppermute | solution.py:14
  19.2 4.1 %copy.28 = f32[1296,8,1]{0,1,2:T(8,128)S(1)} copy(f32[1296,8,1]{2,0,1:T(8,128)} %get-tuple-element.22) | data formatting | bytes 82944 | tf_op jit(solution)/shard_map/slice | solution.py:44
  29.2 6.2 %collective-permute-start.1 = (f32[1296,1,128]{2,0,1:T(8,128)S(1)}, f32[1296,1,128]{2,0,1:T(8,128)S(1)}, u32[]{:S(2)}, u32[]{:S(2)}) collective-permute-start(f32[1296,1,128]{2,0,1:T(8,128)S(1)} %get-tuple-element.20), channel_id=1, source_target_pairs={{4,0},{8,4},{12,8},{16,12},{20,16},{24,20},{28,24},{32,28},{36,32}... | collective-permute-start | bytes 1990664 | tf_op jit(solution)/shard_map/ppermute | solution.py:25
  35.4 9.5 %fusion.63 = (f32[1296,8,127]{2,0,1:T(8,128)}, f32[1296,8,127]{2,0,1:T(8,128)}) fusion(f32[1296,8,128]{2,0,1:T(8,128)} %copy-done.1), kind=kLoop, calls=%fused_computation.131 | loop fusion | bytes 21067776 | tf_op jit(solution)/shard_map/slice | solution.py:50
  52.5 6.5 %collective-permute-done.1 = f32[1296,1,128]{2,0,1:T(8,128)S(1)} collective-permute-done((f32[1296,1,128]{2,0,1:T(8,128)S(1)}, f32[1296,1,128]{2,0,1:T(8,128)S(1)}, u32[]{:S(2)}, u32[]{:S(2)}) %collective-permute-start.1) | collective-permute-done | bytes 663584 | tf_op jit(solution)/shard_map/ppermute | solution.py:25
  59.0 13.1 %convert_bitcast_fusion.1 = (bf16[8,162,8,128]{3,2,1,0:T(8,128)(2,1)S(1)}, f32[1296,8,128]{2,0,1:T(8,128)S(1)}) fusion(f32[1296,8,1]{2,0,1:T(8,128)} %copy.29, f32[1296,8,127]{2,0,1:T(8,128)} %get-tuple-element.24, f32[1296]{0:T(1024)S(1)} %get-tuple-element.35, f32[1296,8,127]{2,0,1:T(8,128)} %get-tuple-element.23, f32[1296,8,1]{2,0,1:T(8,128)} %copy.27, ...), kind=kLoop, calls=%fused_computation.35 | loop fusion | flops 18579456 | bytes 25240896
  72.1 4.3 %multiply_bitcast_fusion.1 = f32[162,8,8,128]{3,2,1,0:T(8,128)S(1)} fusion(bf16[1296,1296]{1,0:T(8,128)(2,1)S(1)} %copy-done.8, bf16[8,162,8,128]{3,2,1,0:T(8,128)(2,1)S(1)} %get-tuple-element.11), kind=kOutput, calls=%fused_computation.29 | convolution fusion | flops 3441180672 | bytes 11321856 | tf_op jit(solution)/shard_map/dot_general | solution.py:64
  77.2 5.7 %fusion.59 = (f32[1296,8,1]{2,0,1:T(8,128)}, f32[1296,8,1]{2,0,1:T(8,128)}) fusion(f32[1296,8,128]{2,0,1:T(8,128)S(1)} %fusion.4), kind=kLoop, calls=%fused_computation.127 | loop fusion | bytes 165888 | tf_op jit(solution)/shard_map/slice | solution.py:43
  83.1 4.1 %copy.32 = f32[1296,8,1]{0,1,2:T(8,128)S(1)} copy(f32[1296,8,1]{2,0,1:T(8,128)} %get-tuple-element.15) | data formatting | bytes 82944 | tf_op jit(solution)/shard_map/slice | solution.py:43
  87.2 4.0 %collective-permute-start.6 = (f32[1296,8,1]{0,1,2:T(8,128)S(1)}, f32[1296,8,1]{0,1,2:T(8,128)S(1)}, u32[]{:S(2)}, u32[]{:S(2)}) collective-permute-start(f32[1296,8,1]{0,1,2:T(8,128)S(1)} %copy.32), channel_id=1, source_target_pairs={{0,1},{1,2},{2,3},{4,5},{5,6},{6,7},{8,9},{9,10},{10,11},{12,13},{... | collective-permute-start | bytes 124424 | tf_op jit(solution)/shard_map/ppermute | solution.py:14
  91.2 4.1 %copy.34 = f32[1296,8,1]{0,1,2:T(8,128)S(1)} copy(f32[1296,8,1]{2,0,1:T(8,128)} %get-tuple-element.16) | data formatting | bytes 82944 | tf_op jit(solution)/shard_map/slice | solution.py:44
  99.8 4.7 %collective-permute-start.5 = (f32[1296,1,128]{2,0,1:T(8,128)S(1)}, f32[1296,1,128]{2,0,1:T(8,128)S(1)}, u32[]{:S(2)}, u32[]{:S(2)}) collective-permute-start(f32[1296,1,128]{2,0,1:T(8,128)S(1)} %get-tuple-element.14), channel_id=1, source_target_pairs={{4,0},{8,4},{12,8},{16,12},{20,16},{24,20},{28,24},{32,28},{36,32}... | collective-permute-start | bytes 1990664 | tf_op jit(solution)/shard_map/ppermute | solution.py:25
  104.5 9.5 %fusion.60 = (f32[1296,8,127]{2,0,1:T(8,128)}, f32[1296,8,127]{2,0,1:T(8,128)}) fusion(f32[1296,8,128]{2,0,1:T(8,128)} %copy-done.2), kind=kLoop, calls=%fused_computation.128 | loop fusion | bytes 21067776 | tf_op jit(solution)/shard_map/slice | solution.py:50
  121.5 7.8 %collective-permute-done.5 = f32[1296,1,128]{2,0,1:T(8,128)S(1)} collective-permute-done((f32[1296,1,128]{2,0,1:T(8,128)S(1)}, f32[1296,1,128]{2,0,1:T(8,128)S(1)}, u32[]{:S(2)}, u32[]{:S(2)}) %collective-permute-start.5) | collective-permute-done | bytes 663584 | tf_op jit(solution)/shard_map/ppermute | solution.py:25
  129.3 13.1 %convert_bitcast_fusion = (bf16[8,162,8,128]{3,2,1,0:T(8,128)(2,1)S(1)}, f32[1296,8,128]{2,0,1:T(8,128)S(1)}) fusion(f32[1296,8,1]{2,0,1:T(8,128)} %copy.35, f32[1296,8,127]{2,0,1:T(8,128)} %get-tuple-element.18, f32[1296]{0:T(1024)S(1)} %get-tuple-element.35, f32[1296,8,127]{2,0,1:T(8,128)} %get-tuple-element.17, f32[1296,8,1]{2,0,1:T(8,128)} %copy.33, ...), kind=kLoop, calls=%fused_computation.34 | loop fusion | flops 18579456 | bytes 25240896
  142.4 4.3 %multiply_bitcast_fusion = f32[162,8,8,128]{3,2,1,0:T(8,128)S(1)} fusion(bf16[1296,1296]{1,0:T(8,128)(2,1)S(1)} %copy-done.9, bf16[8,162,8,128]{3,2,1,0:T(8,128)(2,1)S(1)} %get-tuple-element.9), kind=kOutput, calls=%fused_computation.28 | convolution fusion | flops 3441180672 | bytes 11321856 | tf_op jit(solution)/shard_map/dot_general | solution.py:64
  155.3 4.4 %collective-permute-start.9 = (f32[5,8,128]{2,1,0:T(8,128)S(1)}, f32[5,8,128]{2,1,0:T(8,128)S(1)}, u32[]{:S(2)}, u32[]{:S(2)}) collective-permute-start(f32[5,8,128]{2,1,0:T(8,128)S(1)} %bitcast.57), channel_id=1, source_target_pairs={{4,0},{8,4},{12,8},{16,12},{20,16},{24,20},{28,24},{32,28},{36,32}... | collective-permute-start | bytes 61448 | tf_op jit(solution)/shard_map/ppermute | solution.py:25
  161.6 10.7 %shard_map.121 = f32[5,24,384]{2,1,0:T(8,128)} custom-call(f32[5,24,128]{2,1,0:T(8,128)} %pad_maximum_fusion.31.near_ref, s32[24,4,384]{2,1,0:T(4,128)} %bitcast.54, f32[24,4,384]{2,1,0:T(4,128)} %bitcast.55), custom_call_target="tpu_custom_call" | custom-call | tf_op jit(solution)/shard_map/pallas_call | solution.py:143
  174.0 6.6 %collective-permute-start.11 = (f32[19,1,384]{2,1,0:T(1,128)S(1)}, f32[19,1,384]{2,1,0:T(1,128)S(1)}, u32[]{:S(2)}, u32[]{:S(2)}) collective-permute-start(f32[19,1,384]{2,1,0:T(1,128)S(1)} %get-tuple-element.30), channel_id=1, source_target_pairs={{4,0},{8,4},{12,8},{16,12},{20,16},{24,20},{28,24},{32,28},{36,32}... | collective-permute-start | bytes 87560 | tf_op jit(solution)/shard_map/ppermute | solution.py:25
  180.6 7.4 %copy.39 = f32[1296,8,128]{2,1,0:T(8,128)} copy(f32[1296,8,128]{2,0,1:T(8,128)} %copy-done.3) | data formatting | bytes 10616832
  188.2 6.1 %collective-permute-start.12 = (f32[19,26,1]{2,1,0:T(8,128)S(1)}, f32[19,26,1]{2,1,0:T(8,128)S(1)}, u32[]{:S(2)}, u32[]{:S(2)}) collective-permute-start(f32[19,26,1]{2,1,0:T(8,128)S(1)} %get-tuple-element.28), channel_id=1, source_target_pairs={{0,1},{1,2},{2,3},{4,5},{5,6},{6,7},{8,9},{9,10},{10,11},{12,13},{... | collective-permute-start | bytes 5936 | tf_op jit(solution)/shard_map/ppermute | solution.py:24
  198.1 4.4 %collective-permute-done.13 = f32[19,26,1]{2,1,0:T(8,128)S(1)} collective-permute-done((f32[19,26,1]{2,1,0:T(8,128)S(1)}, f32[19,26,1]{2,1,0:T(8,128)S(1)}, u32[]{:S(2)}, u32[]{:S(2)}) %collective-permute-start.13) | collective-permute-done | bytes 2008 | tf_op jit(solution)/shard_map/ppermute | solution.py:25
  (66 shorter events, 49.2 us)
Async XLA Ops:
  0.6 149.0 %copy-start = (f32[5,1296]{1,0:T(8,128)S(1)}, f32[5,1296]{1,0:T(8,128)}, u32[]{:S(2)}) copy-start(f32[5,1296]{1,0:T(8,128)} %param.13) | copy-start | bytes 77764
  4.9 5.7 %copy-start.1 = (f32[1296,8,128]{2,0,1:T(8,128)}, f32[1296,8,128]{2,0,1:T(8,128)S(1)}, u32[]{:S(2)}) copy-start(f32[1296,8,128]{2,0,1:T(8,128)S(1)} %copy_multiply_fusion) | copy-start | bytes 15925252
  14.7 30.3 %collective-permute-start.2 = (f32[1296,8,1]{0,1,2:T(8,128)S(1)}, f32[1296,8,1]{0,1,2:T(8,128)S(1)}, u32[]{:S(2)}, u32[]{:S(2)}) collective-permute-start(f32[1296,8,1]{0,1,2:T(8,128)S(1)} %copy.26), channel_id=1, source_target_pairs={{0,1},{1,2},{2,3},{4,5},{5,6},{6,7},{8,9},{9,10},{10,11},{12,13},{... | collective-permute-start | bytes 124424 | tf_op jit(solution)/shard_map/ppermute | solution.py:14
  23.3 25.5 %collective-permute-start.3 = (f32[1296,8,1]{0,1,2:T(8,128)S(1)}, f32[1296,8,1]{0,1,2:T(8,128)S(1)}, u32[]{:S(2)}, u32[]{:S(2)}) collective-permute-start(f32[1296,8,1]{0,1,2:T(8,128)S(1)} %copy.28), channel_id=1, source_target_pairs={{1,0},{2,1},{3,2},{5,4},{6,5},{7,6},{9,8},{10,9},{11,10},{13,12},{... | collective-permute-start | bytes 124424 | tf_op jit(solution)/shard_map/ppermute | solution.py:14
  26.7 25.9 %collective-permute-start = (f32[1296,1,128]{2,0,1:T(8,128)S(1)}, f32[1296,1,128]{2,0,1:T(8,128)S(1)}, u32[]{:S(2)}, u32[]{:S(2)}) collective-permute-start(f32[1296,1,128]{2,0,1:T(8,128)S(1)} %get-tuple-element.19), channel_id=1, source_target_pairs={{0,4},{4,8},{8,12},{12,16},{16,20},{20,24},{24,28},{28,32},{32,36}... | collective-permute-start | bytes 1990664 | tf_op jit(solution)/shard_map/ppermute | solution.py:24
  29.2 29.8 %collective-permute-start.1 = (f32[1296,1,128]{2,0,1:T(8,128)S(1)}, f32[1296,1,128]{2,0,1:T(8,128)S(1)}, u32[]{:S(2)}, u32[]{:S(2)}) collective-permute-start(f32[1296,1,128]{2,0,1:T(8,128)S(1)} %get-tuple-element.20), channel_id=1, source_target_pairs={{4,0},{8,4},{12,8},{16,12},{20,16},{24,20},{28,24},{32,28},{36,32}... | collective-permute-start | bytes 1990664 | tf_op jit(solution)/shard_map/ppermute | solution.py:25
  59.0 13.1 %copy-start.8 = (bf16[1296,1296]{1,0:T(8,128)(2,1)S(1)}, bf16[1296,1296]{1,0:T(8,128)(2,1)}, u32[]{:S(2)}) copy-start(bf16[1296,1296]{1,0:T(8,128)(2,1)} %param.12) | copy-start | bytes 10077700
  77.2 5.7 %copy-start.2 = (f32[1296,8,128]{2,0,1:T(8,128)}, f32[1296,8,128]{2,0,1:T(8,128)S(1)}, u32[]{:S(2)}) copy-start(f32[1296,8,128]{2,0,1:T(8,128)S(1)} %fusion.4) | copy-start | bytes 15925252
  87.2 26.9 %collective-permute-start.6 = (f32[1296,8,1]{0,1,2:T(8,128)S(1)}, f32[1296,8,1]{0,1,2:T(8,128)S(1)}, u32[]{:S(2)}, u32[]{:S(2)}) collective-permute-start(f32[1296,8,1]{0,1,2:T(8,128)S(1)} %copy.32), channel_id=1, source_target_pairs={{0,1},{1,2},{2,3},{4,5},{5,6},{6,7},{8,9},{9,10},{10,11},{12,13},{... | collective-permute-start | bytes 124424 | tf_op jit(solution)/shard_map/ppermute | solution.py:14
  95.3 22.5 %collective-permute-start.7 = (f32[1296,8,1]{0,1,2:T(8,128)S(1)}, f32[1296,8,1]{0,1,2:T(8,128)S(1)}, u32[]{:S(2)}, u32[]{:S(2)}) collective-permute-start(f32[1296,8,1]{0,1,2:T(8,128)S(1)} %copy.34), channel_id=1, source_target_pairs={{1,0},{2,1},{3,2},{5,4},{6,5},{7,6},{9,8},{10,9},{11,10},{13,12},{... | collective-permute-start | bytes 124424 | tf_op jit(solution)/shard_map/ppermute | solution.py:14
  97.3 24.2 %collective-permute-start.4 = (f32[1296,1,128]{2,0,1:T(8,128)S(1)}, f32[1296,1,128]{2,0,1:T(8,128)S(1)}, u32[]{:S(2)}, u32[]{:S(2)}) collective-permute-start(f32[1296,1,128]{2,0,1:T(8,128)S(1)} %get-tuple-element.13), channel_id=1, source_target_pairs={{0,4},{4,8},{8,12},{12,16},{16,20},{20,24},{24,28},{28,32},{32,36}... | collective-permute-start | bytes 1990664 | tf_op jit(solution)/shard_map/ppermute | solution.py:24
  99.8 29.5 %collective-permute-start.5 = (f32[1296,1,128]{2,0,1:T(8,128)S(1)}, f32[1296,1,128]{2,0,1:T(8,128)S(1)}, u32[]{:S(2)}, u32[]{:S(2)}) collective-permute-start(f32[1296,1,128]{2,0,1:T(8,128)S(1)} %get-tuple-element.14), channel_id=1, source_target_pairs={{4,0},{8,4},{12,8},{16,12},{20,16},{24,20},{28,24},{32,28},{36,32}... | collective-permute-start | bytes 1990664 | tf_op jit(solution)/shard_map/ppermute | solution.py:25
  129.3 13.1 %copy-start.9 = (bf16[1296,1296]{1,0:T(8,128)(2,1)S(1)}, bf16[1296,1296]{1,0:T(8,128)(2,1)}, u32[]{:S(2)}) copy-start(bf16[1296,1296]{1,0:T(8,128)(2,1)} %param.12) | copy-start | bytes 10077700
  147.3 2.3 %copy-start.3 = (f32[1296,8,128]{2,0,1:T(8,128)}, f32[1296,8,128]{2,0,1:T(8,128)S(1)}, u32[]{:S(2)}) copy-start(f32[1296,8,128]{2,0,1:T(8,128)S(1)} %fusion.3) | copy-start | bytes 15925252
  149.6 10.2 %copy-start.7 = (f32[384]{0:T(512)S(1)}, f32[384]{0:T(512)}, u32[]{:S(2)}) copy-start(f32[384]{0:T(512)} %param.19) | copy-start | bytes 4612
  149.6 23.5 %copy-start.4 = (f32[8,24,384]{2,1,0:T(8,128)S(1)}, f32[8,24,384]{2,1,0:T(8,128)}, u32[]{:S(2)}) copy-start(f32[8,24,384]{2,1,0:T(8,128)} %param.17) | copy-start | bytes 884740
  149.6 23.6 %copy-start.5 = (f32[8,24,384]{2,1,0:T(8,128)S(1)}, f32[8,24,384]{2,1,0:T(8,128)}, u32[]{:S(2)}) copy-start(f32[8,24,384]{2,1,0:T(8,128)} %param.16) | copy-start | bytes 884740
  149.6 31.0 %copy-start.6 = (s32[24,384]{1,0:T(8,128)S(1)}, s32[24,384]{1,0:T(8,128)}, u32[]{:S(2)}) copy-start(s32[24,384]{1,0:T(8,128)} %param.18) | copy-start | bytes 110596
  152.5 8.4 %collective-permute-start.8 = (f32[5,8,128]{2,1,0:T(8,128)S(1)}, f32[5,8,128]{2,1,0:T(8,128)S(1)}, u32[]{:S(2)}, u32[]{:S(2)}) collective-permute-start(f32[5,8,128]{2,1,0:T(8,128)S(1)} %bitcast.56), channel_id=1, source_target_pairs={{0,4},{4,8},{8,12},{12,16},{16,20},{20,24},{24,28},{28,32},{32,36}... | collective-permute-start | bytes 61448 | tf_op jit(solution)/shard_map/ppermute | solution.py:24
  155.3 5.6 %collective-permute-start.9 = (f32[5,8,128]{2,1,0:T(8,128)S(1)}, f32[5,8,128]{2,1,0:T(8,128)S(1)}, u32[]{:S(2)}, u32[]{:S(2)}) collective-permute-start(f32[5,8,128]{2,1,0:T(8,128)S(1)} %bitcast.57), channel_id=1, source_target_pairs={{4,0},{8,4},{12,8},{16,12},{20,16},{24,20},{28,24},{32,28},{36,32}... | collective-permute-start | bytes 61448 | tf_op jit(solution)/shard_map/ppermute | solution.py:25
  173.2 14.7 %collective-permute-start.10 = (f32[19,1,384]{2,1,0:T(1,128)S(1)}, f32[19,1,384]{2,1,0:T(1,128)S(1)}, u32[]{:S(2)}, u32[]{:S(2)}) collective-permute-start(f32[19,1,384]{2,1,0:T(1,128)S(1)} %get-tuple-element.29), channel_id=1, source_target_pairs={{0,4},{4,8},{8,12},{12,16},{16,20},{20,24},{24,28},{28,32},{32,36}... | collective-permute-start | bytes 87560 | tf_op jit(solution)/shard_map/ppermute | solution.py:24
  174.0 14.0 %collective-permute-start.11 = (f32[19,1,384]{2,1,0:T(1,128)S(1)}, f32[19,1,384]{2,1,0:T(1,128)S(1)}, u32[]{:S(2)}, u32[]{:S(2)}) collective-permute-start(f32[19,1,384]{2,1,0:T(1,128)S(1)} %get-tuple-element.30), channel_id=1, source_target_pairs={{4,0},{8,4},{12,8},{16,12},{20,16},{24,20},{28,24},{32,28},{36,32}... | collective-permute-start | bytes 87560 | tf_op jit(solution)/shard_map/ppermute | solution.py:25
  188.2 9.9 %collective-permute-start.12 = (f32[19,26,1]{2,1,0:T(8,128)S(1)}, f32[19,26,1]{2,1,0:T(8,128)S(1)}, u32[]{:S(2)}, u32[]{:S(2)}) collective-permute-start(f32[19,26,1]{2,1,0:T(8,128)S(1)} %get-tuple-element.28), channel_id=1, source_target_pairs={{0,1},{1,2},{2,3},{4,5},{5,6},{6,7},{8,9},{9,10},{10,11},{12,13},{... | collective-permute-start | bytes 5936 | tf_op jit(solution)/shard_map/ppermute | solution.py:24
  194.3 8.2 %collective-permute-start.13 = (f32[19,26,1]{2,1,0:T(8,128)S(1)}, f32[19,26,1]{2,1,0:T(8,128)S(1)}, u32[]{:S(2)}, u32[]{:S(2)}) collective-permute-start(f32[19,26,1]{2,1,0:T(8,128)S(1)} %get-tuple-element.27), channel_id=1, source_target_pairs={{1,0},{2,1},{3,2},{5,4},{6,5},{7,6},{9,8},{10,9},{11,10},{13,12},{... | collective-permute-start | bytes 5936 | tf_op jit(solution)/shard_map/ppermute | solution.py:25

commit v2 on v0

v2 whole, which is shorter than its diff:
```python
import math

import jax
import jax.numpy as jnp
from jax import lax
from jax.experimental import pallas as pl
from jax.experimental.pallas import tpu as pltpu
from jax.sharding import PartitionSpec as P

NFREQ = 36
MESH = pl.DeviceIdType.MESH
VMEM = pl.BlockSpec(memory_space=pltpu.VMEM)
ANY = pl.BlockSpec(memory_space=pl.ANY)
LANES = 128
PAIR = 16
GRANT = 60 * 1024 * 1024


def courant(components, freqs):
    index = jnp.arange(components, dtype=jnp.int32)
    direction = (index // freqs).astype(jnp.float32)
    level = (index % freqs).astype(jnp.float32)
    theta = 2.0 * jnp.pi * (direction + 0.5) / (components // freqs)
    speed = jnp.power(jnp.float32(1.1), -level)
    east = 0.45 * speed * jnp.cos(theta)
    north = 0.45 * speed * jnp.sin(theta)
    return jnp.stack(
        [
            1.0 - jnp.abs(east) - jnp.abs(north),
            jnp.abs(east),
            jnp.abs(north),
            jnp.maximum(east, 0.0),
            jnp.maximum(-east, 0.0),
            jnp.maximum(north, 0.0),
            jnp.maximum(-north, 0.0),
            jnp.zeros_like(east),
        ],
        axis=1,
    )


def sign_of(function, first, last, freqs, directions):
    signs = set()
    for d in range(first // freqs, (last - 1) // freqs + 1):
        signs.add(1 if function(2 * math.pi * (d + 0.5) / directions) > 0 else -1)
    return signs.pop() if len(signs) == 1 else 0


def segments(components, freqs):
    directions = components // freqs
    runs = []
    for pair in range(components // PAIR):
        first, last = pair * PAIR, (pair + 1) * PAIR
        key = (
            sign_of(math.cos, first, last, freqs, directions),
            sign_of(math.sin, first, last, freqs, directions),
        )
        if runs and runs[-1][2] == key:
            runs[-1][1] = pair + 1
        else:
            runs.append([pair, pair + 1, key])
    return [(a, b, xs, ys) for a, b, (xs, ys) in runs]


def row_spans(components, freqs, sign):
    spans = []
    for a, b, xs, _ in segments(components, freqs):
        if xs == -sign:
            continue
        if spans and spans[-1][1] == a * PAIR:
            spans[-1][1] = b * PAIR
        else:
            spans.append([a * PAIR, b * PAIR])
    return [tuple(s) for s in spans]


def complement(spans, total):
    out, at = [], 0
    for a, b in spans:
        if a > at:
            out.append((at, a))
        at = b
    if at < total:
        out.append((at, total))
    return out


def south_lane(c):
    return 2 * c + 1 if 0 <= c < 8 else (32 if c < 0 else 33)


def north_lane(c):
    return 16 + 2 * c if 0 <= c < 8 else (34 if c < 0 else 35)


def lane_shift(x, source, target):
    return pltpu.roll(x, (target - source) % LANES, 1)


def coefficients(coef, xs, ys):
    def wide(n):
        return jnp.broadcast_to(coef[:, n : n + 1], (PAIR, LANES))

    return dict(
        c=wide(0),
        x=wide(1) if xs else (wide(3), wide(4)),
        y=wide(2) if ys else (wide(5), wide(6)),
    )


def upwind(co, xs, ys, centre, west, east, south, north):
    result = co["c"] * centre
    if xs:
        result = result + co["x"] * (west() if xs > 0 else east())
    else:
        result = result + co["x"][0] * west() + co["x"][1] * east()
    if ys:
        result = result + co["y"] * (south() if ys > 0 else north())
    else:
        result = result + co["y"][0] * south() + co["y"][1] * north()
    return result


def advect_columns(co, xs, ys, columns, state, ghost, lane):
    out = {}
    for c in columns:
        out[c] = upwind(
            co,
            xs,
            ys,
            state[c],
            lambda: state[c - 1],
            lambda: state[c + 1],
            lambda: jnp.where(
                lane == 0, lane_shift(ghost, south_lane(c), 0), pltpu.roll(state[c], 1, 1)
            ),
            lambda: jnp.where(
                lane == LANES - 1,
                lane_shift(ghost, north_lane(c), LANES - 1),
                pltpu.roll(state[c], LANES - 1, 1),
            ),
        )
    return out


def needed(columns, xs):
    want = set(columns)
    if xs >= 0:
        want |= {c - 1 for c in columns}
    if xs <= 0:
        want |= {c + 1 for c in columns}
    return sorted(want)


def over_rows(runs, body):
    for a, b, xs, ys in runs:
        if b - a == 1:
            body(a * PAIR, xs, ys)
        else:
            def step(p, carry, xs=xs, ys=ys):
                body(pl.multiple_of(p * PAIR, PAIR), xs, ys)
                return carry

            lax.fori_loop(a, b, step, 0)


def wave_kernel(
    spectrum, sea, transfer, coef_hbm, cell_hbm, weight_hbm, u_hbm, v_hbm,
    x1_out, ghost_out, cells_out, weights_out, rows_out, cols_out,
    x, a, ab, abe, t, coef, masks, sides, packed, turned, gturned, g, ga,
    cell, weight, u, v, cells, weights, rows_send, cols_send, rows_in, cols_in,
    local_sem, send_sem, recv_sem, out_sem,
):
    lon, lat = lax.axis_index("lon"), lax.axis_index("lat")
    nlon, nlat = lax.axis_size("lon"), lax.axis_size("lat")
    components, width, _ = spectrum.shape
    runs = segments(components, NFREQ)
    plus = row_spans(components, NFREQ, 1)
    minus = row_spans(components, NFREQ, -1)
    east, west = lax.rem(lon + 1, nlon), lax.rem(lon + nlon - 1, nlon)
    has_south, has_north = lat > 0, lat < nlat - 1
    lane = lax.broadcasted_iota(jnp.int32, (PAIR, LANES), 1)

    gturned[...] = jnp.zeros_like(gturned)
    cols_in[...] = jnp.zeros_like(cols_in)

    local = []

    def load(src, dst):
        copy = pltpu.make_async_copy(src, dst, local_sem.at[len(local)])
        copy.start()
        local.append(copy)
        return copy

    barrier = pltpu.get_barrier_semaphore()

    def greet(to_lon, to_lat):
        pl.semaphore_signal(barrier, inc=1, device_id=(to_lon, to_lat), device_id_type=MESH)

    greet(east, lat)
    greet(west, lat)

    @pl.when(has_north)
    def _():
        greet(lon, lat + 1)
        greet(east, lat + 1)
        greet(west, lat + 1)

    @pl.when(has_south)
    def _():
        greet(lon, lat - 1)
        greet(east, lat - 1)
        greet(west, lat - 1)

    columns_in = [load(spectrum.at[:, c, :], x.at[c + 2]) for c in range(width)]
    coef_in = load(coef_hbm, coef)
    cell_in = load(cell_hbm, cell)
    weight_in = load(weight_hbm, weight)
    u_in = load(u_hbm, u)
    v_in = load(v_hbm, v)
    transfer_in = load(transfer, t)

    pl.semaphore_wait(
        barrier, 2 + 3 * has_north.astype(jnp.int32) + 3 * has_south.astype(jnp.int32)
    )

    count = [0]

    def remote(src, dst, to_lon, to_lat):
        n = count[0]
        count[0] += 1
        return pltpu.make_async_remote_copy(
            src_ref=src,
            dst_ref=dst,
            send_sem=send_sem.at[n],
            recv_sem=recv_sem.at[n],
            device_id=(to_lon, to_lat),
            device_id_type=MESH,
        )

    def columns(spans, column, slot, to_lon):
        return [
            remote(
                spectrum.at[pl.ds(k0, k1 - k0), column, :],
                x.at[slot, pl.ds(k0, k1 - k0), :],
                to_lon,
                lat,
            )
            for k0, k1 in spans
        ]

    first = columns(plus, width - 1, 1, east) + columns(minus, 0, width + 2, west)
    second = (
        columns(complement(plus, components), width - 1, 1, east)
        + columns(plus, width - 2, 0, east)
        + columns(complement(minus, components), 0, width + 2, west)
        + columns(minus, 1, width + 3, west)
    )
    side_masks = [remote(sea, sides.at[0], east, lat), remote(sea, sides.at[1], west, lat)]
    for copy in side_masks + first:
        copy.start()

    for c in range(width):
        masks[c + 2] = jnp.broadcast_to(
            sea[pl.ds(c, 1), :].astype(jnp.float32), (PAIR, LANES)
        )

    for copy in columns_in:
        copy.wait()

    def pack(r, values):
        total = jnp.zeros((PAIR, LANES), jnp.float32)
        half = lane // 2
        for c in range(width):
            total = jnp.where(half == c, lane_shift(values[c], LANES - 2, 2 * c), total)
            total = jnp.where(half == 8 + c, lane_shift(values[c], 0, 16 + 2 * c), total)
        packed[pl.ds(r, PAIR), :] = total

    def pack_rows(p, carry):
        r = pl.multiple_of(p * PAIR, PAIR)
        pack(r, [x[c + 2, pl.ds(r, PAIR), :] * masks[c + 2] for c in range(width)])
        return carry

    lax.fori_loop(0, components // PAIR, pack_rows, 0)
    pack(components, [masks[c + 2] for c in range(width)])
    blocks = packed.shape[0] // LANES
    tail = components + PAIR
    packed[pl.ds(tail, blocks * LANES - tail), :] = jnp.zeros(
        (blocks * LANES - tail, LANES), jnp.float32
    )
    for b in range(blocks):
        turned[:, b * LANES : (b + 1) * LANES] = jnp.transpose(
            packed[b * LANES : (b + 1) * LANES, :]
        )[:32, :]

    for copy in (cell_in, weight_in, u_in, v_in):
        copy.wait()
    height, taps, length = cell.shape
    for i in range(height):
        for tap in range(taps):
            cells[tap, pl.ds(i, 1), :] = cell[i, pl.ds(tap, 1), :]
            weights[tap, pl.ds(i, 1), :] = weight[i, pl.ds(tap, 1), :]
    levels = u.shape[0]
    for side, row in ((0, height - 1), (1, 0)):
        for level in range(levels):
            rows_send[side, pl.ds(level, 1), :] = u[level, pl.ds(row, 1), :]
            rows_send[side, pl.ds(levels + level, 1), :] = v[level, pl.ds(row, 1), :]
        for tap in range(taps):
            rows_send[side, pl.ds(2 * levels + tap, 1), :] = weights[tap, pl.ds(row, 1), :]
            rows_send[side, pl.ds(2 * levels + taps + tap, 1), :] = cells[
                tap, pl.ds(row, 1), :
            ].astype(jnp.float32)
    lane_all = lax.broadcasted_iota(jnp.int32, (height, LANES), 1)
    for side, start, source in ((0, length - LANES, LANES - 1), (1, 0, 0)):
        total = jnp.zeros((height, LANES), jnp.float32)
        for n in range(2 * levels + 2 * taps):
            if n < levels:
                block = u[n, :, start : start + LANES]
            elif n < 2 * levels:
                block = v[n - levels, :, start : start + LANES]
            elif n < 2 * levels + taps:
                block = weights[n - 2 * levels, :, start : start + LANES]
            else:
                block = cells[n - 2 * levels - taps, :, start : start + LANES].astype(jnp.float32)
            total = jnp.where(lane_all == n, lane_shift(block, source, n), total)
        cols_send[side] = total

    rows_copy = [
        remote(rows_send.at[0], rows_in.at[0], east, lat),
        remote(rows_send.at[1], rows_in.at[1], west, lat),
    ]
    to_north = [
        remote(turned.at[pl.ds(0, 16), :], gturned.at[pl.ds(0, 16), :], lon, lat + 1),
        remote(turned.at[pl.ds(15, 1), :], gturned.at[pl.ds(32, 1), :], east, lat + 1),
        remote(turned.at[pl.ds(1, 1), :], gturned.at[pl.ds(33, 1), :], west, lat + 1),
        remote(cols_send.at[0], cols_in.at[0], lon, lat + 1),
    ]
    to_south = [
        remote(turned.at[pl.ds(16, 16), :], gturned.at[pl.ds(16, 16), :], lon, lat - 1),
        remote(turned.at[pl.ds(30, 1), :], gturned.at[pl.ds(34, 1), :], east, lat - 1),
        remote(turned.at[pl.ds(16, 1), :], gturned.at[pl.ds(35, 1), :], west, lat - 1),
        remote(cols_send.at[1], cols_in.at[1], lon, lat - 1),
    ]

    @pl.when(has_north)
    def _():
        for copy in to_north:
            copy.start()

    @pl.when(has_south)
    def _():
        for copy in to_south:
            copy.start()

    for copy in rows_copy + second:
        copy.start()

    stores = []

    def store(src, dst):
        copy = pltpu.make_async_copy(src, dst, out_sem.at[len(stores)])
        copy.start()
        stores.append(copy)

    store(cells, cells_out)
    store(weights, weights_out)

    for copy in side_masks + first:
        copy.wait_recv()

    @pl.when(has_south)
    def _():
        for copy in to_north:
            copy.wait_recv()

    @pl.when(has_north)
    def _():
        for copy in to_south:
            copy.wait_recv()

    for slot, side, row in ((0, 0, width - 2), (1, 0, width - 1), (width + 2, 1, 0), (width + 3, 1, 1)):
        masks[slot] = jnp.broadcast_to(
            sides[side, pl.ds(row, 1), :].astype(jnp.float32), (PAIR, LANES)
        )
    for b in range(blocks):
        g[b * LANES : (b + 1) * LANES, :] = jnp.transpose(
            gturned[:, b * LANES : (b + 1) * LANES]
        )
    coef_in.wait()
    own = list(range(width))

    def first_step(r, xs, ys):
        co = coefficients(coef[pl.ds(r, PAIR), :], xs, ys)
        state = {c: x[c + 2, pl.ds(r, PAIR), :] * masks[c + 2] for c in needed(own, xs)}
        ghost = g[pl.ds(r, PAIR), :]
        mine = packed[pl.ds(r, PAIR), :]
        for c, value in advect_columns(co, xs, ys, own, state, ghost, lane).items():
            a[c + 1, pl.ds(r, PAIR), :] = value
            ab[pl.ds(r, PAIR), c * LANES : (c + 1) * LANES] = value.astype(jnp.bfloat16)

        def sideways(step, low, high):
            moved = pltpu.roll(ghost, step % LANES, 1)
            for target, source in (low, high):
                moved = jnp.where(lane == target, lane_shift(ghost, source, target), moved)
            return moved

        value = upwind(
            co,
            xs,
            ys,
            ghost,
            lambda: sideways(2, (1, 32), (16, 34)),
            lambda: sideways(-2, (15, 33), (30, 35)),
            lambda: jnp.where(lane < 16, pltpu.roll(ghost, 1, 1), pltpu.roll(mine, 15, 1)),
            lambda: jnp.where(
                lane < 16, pltpu.roll(mine, LANES - 15, 1), pltpu.roll(ghost, LANES - 1, 1)
            ),
        )
        ga[pl.ds(r, PAIR), :] = value
        ab[pl.ds(r, PAIR), width * LANES : (width + 1) * LANES] = value.astype(jnp.bfloat16)

    over_rows(runs, first_step)
    transfer_in.wait()
    block = 432
    ghost_mask = g[pl.ds(components, 1), :]

    def product(m, carry):
        r = pl.multiple_of(m * block, PAIR)
        rows = pl.ds(r, block)
        for n in range(0, width, 2):
            added = jnp.dot(
                t[rows, :],
                ab[:, n * LANES : (n + 2) * LANES],
                preferred_element_type=jnp.float32,
            )
            for c in (n, n + 1):
                part = added[:, (c - n) * LANES : (c - n + 1) * LANES]
                a[c + 1, rows, :] = masks[c + 2, pl.ds(0, 1), :] * (a[c + 1, rows, :] + 0.5 * part)
        added = jnp.dot(
            t[rows, :],
            ab[:, width * LANES : (width + 1) * LANES],
            preferred_element_type=jnp.float32,
        )
        ga[rows, :] = ghost_mask * (ga[rows, :] + 0.5 * added)
        return carry

    lax.fori_loop(0, components // block, product, 0)
    for c in range(width):
        store(a.at[c + 1], x1_out.at[c + 1])
    store(ga, ghost_out)

    for copy in rows_copy + second:
        copy.wait_recv()
    store(rows_in, rows_out)
    store(cols_in, cols_out)

    outer = [-1, width]

    def outer_step(r, xs, ys):
        co = coefficients(coef[pl.ds(r, PAIR), :], xs, ys)
        state = {c: x[c + 2, pl.ds(r, PAIR), :] * masks[c + 2] for c in needed(outer, xs)}
        ghost = g[pl.ds(r, PAIR), :]
        for c, value in advect_columns(co, xs, ys, outer, state, ghost, lane).items():
            slot = 0 if c < 0 else 1
            a[c + 1, pl.ds(r, PAIR), :] = value
            abe[pl.ds(r, PAIR), slot * LANES : (slot + 1) * LANES] = value.astype(jnp.bfloat16)

    over_rows(runs, outer_step)
    for slot, c, spans in ((0, -1, plus), (1, width, minus)):
        for k0, k1 in spans:
            rows = pl.ds(k0, k1 - k0)
            added = jnp.dot(
                t[rows, :],
                abe[:, slot * LANES : (slot + 1) * LANES],
                preferred_element_type=jnp.float32,
            )
            a[c + 1, rows, :] = masks[c + 2, pl.ds(0, 1), :] * (a[c + 1, rows, :] + 0.5 * added)
            store(a.at[c + 1, rows, :], x1_out.at[c + 1, rows, :])

    for copy in side_masks + first + rows_copy + second:
        copy.wait_send()

    @pl.when(has_north)
    def _():
        for copy in to_north:
            copy.wait_send()

    @pl.when(has_south)
    def _():
        for copy in to_south:
            copy.wait_send()

    for copy in stores:
        copy.wait()


def second_kernel(
    x1_hbm, ghost_hbm, sea, transfer, coef_hbm, bulk_hbm, out, bulk_ref,
    x, a, ab, t, coef, bulk_weight, g, local_sem, out_sem,
):
    width = sea.shape[0]
    components = coef.shape[0]
    runs = segments(components, NFREQ)
    lane = lax.broadcasted_iota(jnp.int32, (PAIR, LANES), 1)
    local = []

    def load(src, dst):
        copy = pltpu.make_async_copy(src, dst, local_sem.at[len(local)])
        copy.start()
        local.append(copy)

    load(coef_hbm, coef)
    load(ghost_hbm, g)
    for c in range(-1, width + 1):
        if c < 0 or c == width:
            for k0, k1 in row_spans(components, NFREQ, 1 if c < 0 else -1):
                rows = pl.ds(k0, k1 - k0)
                load(x1_hbm.at[c + 1, rows, :], x.at[c + 1, rows, :])
        else:
            load(x1_hbm.at[c + 1], x.at[c + 1])
    waits = list(local)
    load(transfer, t)
    load(bulk_hbm, bulk_weight)
    for copy in waits:
        copy.wait()
    own = list(range(width))

    def step(r, xs, ys):
        co = coefficients(coef[pl.ds(r, PAIR), :], xs, ys)
        state = {c: x[c + 1, pl.ds(r, PAIR), :] for c in needed(own, xs)}
        ghost = g[pl.ds(r, PAIR), :]
        for c, value in advect_columns(co, xs, ys, own, state, ghost, lane).items():
            a[c, pl.ds(r, PAIR), :] = value
            ab[pl.ds(r, PAIR), c * LANES : (c + 1) * LANES] = value.astype(jnp.bfloat16)

    over_rows(runs, step)
    for copy in local[len(waits) :]:
        copy.wait()
    block = 432
    stores = []
    for m in range(components // block):
        rows = pl.ds(m * block, block)
        for n in range(0, width, 2):
            added = jnp.dot(
                t[rows, :],
                ab[:, n * LANES : (n + 2) * LANES],
                preferred_element_type=jnp.float32,
            )
            for c in (n, n + 1):
                part = added[:, (c - n) * LANES : (c - n + 1) * LANES]
                wet = sea[pl.ds(c, 1), :].astype(jnp.float32)
                a[c, rows, :] = wet * (a[c, rows, :] + 0.5 * part)
        for c in range(width):
            copy = pltpu.make_async_copy(
                a.at[c, rows, :], out.at[rows, c, :], out_sem.at[len(stores)]
            )
            copy.start()
            stores.append(copy)
    quantities = bulk_ref.shape[0]
    half = width // 2
    for c0 in range(0, width, half):

        def gather(k, totals):
            r = pl.multiple_of(k * 8, 8)
            line = bulk_weight[pl.ds(r, 8), :]
            totals = list(totals)
            wide = [jnp.broadcast_to(line[:, q : q + 1], (8, LANES)) for q in range(quantities)]
            for c in range(half):
                state = a[c0 + c, pl.ds(r, 8), :]
                for q in range(quantities):
                    totals[c * quantities + q] = totals[c * quantities + q] + wide[q] * state
            return tuple(totals)

        zero = jnp.zeros((8, LANES), jnp.float32)
        totals = lax.fori_loop(0, components // 8, gather, (zero,) * (half * quantities))
        for c in range(half):
            for q in range(quantities):
                bulk_ref[q, pl.ds(c0 + c, 1), :] = jnp.sum(
                    totals[c * quantities + q], axis=0, keepdims=True
                )
    for copy in stores:
        copy.wait()


def spread_kernel(bulk, near_out, sides_out, far_out, send_sem, recv_sem):
    lon, lat = lax.axis_index("lon"), lax.axis_index("lat")
    nlon, nlat = lax.axis_size("lon"), lax.axis_size("lat")
    around = [lax.rem(lon + d + nlon, nlon) for d in (-2, -1, 0, 1, 2)]
    has_south, has_north = lat > 0, lat < nlat - 1
    sides_out[...] = jnp.zeros_like(sides_out)
    barrier = pltpu.get_barrier_semaphore()

    def greet(to_lon, to_lat):
        pl.semaphore_signal(barrier, inc=1, device_id=(to_lon, to_lat), device_id_type=MESH)

    for d in (0, 1, 3, 4):
        greet(around[d], lat)

    @pl.when(has_north)
    def _():
        for d in (1, 2, 3):
            greet(around[d], lat + 1)

    @pl.when(has_south)
    def _():
        for d in (1, 2, 3):
            greet(around[d], lat - 1)

    pl.semaphore_wait(
        barrier, 4 + 3 * has_north.astype(jnp.int32) + 3 * has_south.astype(jnp.int32)
    )
    count = [0]

    def remote(src, dst, to_lon, to_lat):
        n = count[0]
        count[0] += 1
        return pltpu.make_async_remote_copy(
            src_ref=src,
            dst_ref=dst,
            send_sem=send_sem.at[n],
            recv_sem=recv_sem.at[n],
            device_id=(to_lon, to_lat),
            device_id_type=MESH,
        )

    drift = bulk.at[pl.ds(1, 2)]
    stress = bulk.at[pl.ds(0, 2)]
    flat = [
        remote(bulk, near_out.at[2], around[1], lat),
        remote(bulk, near_out.at[0], around[3], lat),
        remote(stress, far_out.at[1], around[0], lat),
        remote(stress, far_out.at[0], around[4], lat),
    ]
    to_north = [
        remote(drift, sides_out.at[0, 2], around[1], lat + 1),
        remote(drift, sides_out.at[0, 1], around[2], lat + 1),
        remote(drift, sides_out.at[0, 0], around[3], lat + 1),
    ]
    to_south = [
        remote(drift, sides_out.at[1, 2], around[1], lat - 1),
        remote(drift, sides_out.at[1, 1], around[2], lat - 1),
        remote(drift, sides_out.at[1, 0], around[3], lat - 1),
    ]
    for copy in flat:
        copy.start()

    @pl.when(has_north)
    def _():
        for copy in to_north:
            copy.start()

    @pl.when(has_south)
    def _():
        for copy in to_south:
            copy.start()

    near_out[1] = bulk[...]

    for copy in flat:
        copy.wait()

    @pl.when(has_north)
    def _():
        for copy in to_north:
            copy.wait_send()
        for copy in to_south:
            copy.wait_recv()

    @pl.when(has_south)
    def _():
        for copy in to_south:
            copy.wait_send()
        for copy in to_north:
            copy.wait_recv()


def taken_from(sources, codes, quantities):
    places = [c & (LANES - 1) for c in codes]
    offsets = [c >> 9 for c in codes]
    taken = [[jnp.zeros(codes[0].shape, jnp.float32)] * len(quantities) for _ in codes]
    for o in range(17):
        hits = [offset == o for offset in offsets]
        for n, q in enumerate(quantities):
            source = sources(q, o)
            for i in range(len(codes)):
                got = jnp.take_along_axis(source, places[i], axis=1, mode="promise_in_bounds")
                taken[i][n] = jnp.where(hits[i], got, taken[i][n])
    return taken


def ocean_kernel(
    near, sides, far, cells, weights, rows_in, cols_in, u, v, sea, coriolis, u_out, v_out,
    near1, near3, sides3, forcing, edge_code, edge_weight, edge_rows,
):
    quantities = near.shape[1]
    width = near.shape[2]
    taps, height, length = cells.shape
    levels = u.shape[0]
    for part in range(3):
        near1[:, pl.ds(8 + part * width, width), :] = near[part]
    near1[pl.ds(0, 2), pl.ds(7, 1), :] = far[0, :, pl.ds(width - 1, 1), :]
    near1[pl.ds(0, 2), pl.ds(8 + 3 * width, 1), :] = far[1, :, pl.ds(0, 1), :]
    for i in range(3 * width):
        for q in range(quantities):
            near3[q, pl.ds(3 * i, 3), :] = jnp.broadcast_to(
                near1[q, pl.ds(8 + i, 1), :], (3, LANES)
            )
        for side in range(2):
            for q in range(2):
                sides3[side, q, pl.ds(3 * i, 3), :] = jnp.broadcast_to(
                    sides[side, i // width, q, pl.ds(i % width, 1), :], (3, LANES)
                )

    def block(jb, carry):
        lanes = pl.ds(pl.multiple_of(jb * LANES, LANES), LANES)
        for i0 in range(0, height, 8):
            rows = pl.ds(i0, 8)
            taken = taken_from(
                lambda q, o: near3[q, pl.ds(i0 + 3 * o, 8), :],
                [cells[tap, rows, lanes] for tap in range(taps)],
                range(quantities),
            )
            for q in range(quantities):
                total = 0.0
                for tap in range(taps):
                    total = total + taken[tap][q] * weights[tap, rows, lanes]
                forcing[q, rows, lanes] = total
        low = lax.broadcasted_iota(jnp.int32, (8, LANES), 0) < 4
        taken = taken_from(
            lambda q, o: jnp.where(
                low,
                jnp.broadcast_to(near1[q, pl.ds(7 + o, 1), :], (8, LANES)),
                jnp.broadcast_to(near1[q, pl.ds(16 + o, 1), :], (8, LANES)),
            ),
            [edge_code[:, lanes].astype(jnp.int32)],
            range(2),
        )
        for q in range(2):
            product = taken[0][q] * edge_weight[:, lanes]
            zero = jnp.zeros_like(product)
            edge_rows[q, pl.ds(0, 1), lanes] = jnp.sum(
                jnp.where(low, product, zero), axis=0, keepdims=True
            )
            edge_rows[q, pl.ds(1, 1), lanes] = jnp.sum(
                jnp.where(low, zero, product), axis=0, keepdims=True
            )
        return carry

    for side in range(2):
        edge_code[pl.ds(4 * side, 4), :] = rows_in[side, pl.ds(2 * levels + taps, taps), :]
        edge_weight[pl.ds(4 * side, 4), :] = rows_in[side, pl.ds(2 * levels, taps), :]
    lax.fori_loop(0, length // LANES, block, 0)

    lane = lax.broadcasted_iota(jnp.int32, (8, LANES), 1)
    here = jnp.logical_and(lane >= 2 * levels + taps, lane < 2 * levels + 2 * taps)
    edge_cols = [[], []]
    for side in range(2):
        parts = [[], []]
        for i0 in range(0, height, 8):
            line = cols_in[side, pl.ds(i0, 8), :]
            code = jnp.where(here, line, 0.0).astype(jnp.int32)
            taken = taken_from(
                lambda q, o: sides3[side, q, pl.ds(i0 + 3 * o, 8), :], [code], range(2)
            )
            weight = jnp.where(here, pltpu.roll(line, taps, 1), 0.0)
            for q in range(2):
                parts[q].append(jnp.sum(taken[0][q] * weight, axis=1, keepdims=True))
        for q in range(2):
            edge_cols[side].append(jnp.concatenate(parts[q], axis=0))

    row = lax.broadcasted_iota(jnp.int32, (height, length), 0)
    col = lax.broadcasted_iota(jnp.int32, (height, length), 1)

    def shifted(q, west, east, south, north):
        return (
            jnp.where(row == 0, west, pltpu.roll(q, 1, 0)),
            jnp.where(row == height - 1, east, pltpu.roll(q, height - 1, 0)),
            jnp.where(col == 0, south, pltpu.roll(q, 1, 1)),
            jnp.where(col == length - 1, north, pltpu.roll(q, length - 1, 1)),
        )

    def dx(q, index):
        low = jnp.where(row == 0, edge_rows[index, pl.ds(0, 1), :], pltpu.roll(q, 1, 0))
        high = jnp.where(
            row == height - 1, edge_rows[index, pl.ds(1, 1), :], pltpu.roll(q, height - 1, 0)
        )
        return 0.5 * (high - low)

    def dy(q, index):
        low = jnp.where(col == 0, edge_cols[0][index], pltpu.roll(q, 1, 1))
        high = jnp.where(col == length - 1, edge_cols[1][index], pltpu.roll(q, length - 1, 1))
        return 0.5 * (high - low)

    sxx, sxy, syy = forcing[0], forcing[1], forcing[2]
    force_x = -(dx(sxx, 0) + dy(sxy, 0))
    force_y = -(dx(sxy, 1) + dy(syy, 1))
    wet = sea[...].astype(jnp.float32)
    turn = jnp.broadcast_to(0.5 * coriolis[...], (height, length))
    for level in range(levels):
        decay = math.exp(-level / 3.0)
        here_u, here_v = u[level], v[level]

        def laplace(q, n):
            west, east, south, north = shifted(
                q,
                rows_in[0, pl.ds(n, 1), :],
                rows_in[1, pl.ds(n, 1), :],
                cols_in[0, :, n : n + 1],
                cols_in[1, :, n : n + 1],
            )
            return east + west + north + south - 4.0 * q

        u_out[level] = wet * (
            here_u
            + turn * (here_v + decay * forcing[4])
            + (0.5 * decay) * force_x
            + 0.1 * laplace(here_u, level)
        )
        v_out[level] = wet * (
            here_v
            - turn * (here_u + decay * forcing[3])
            + (0.5 * decay) * force_y
            + 0.1 * laplace(here_v, levels + level)
        )


def local(
    spectrum,
    sea_mask,
    transfer,
    bulk_weight,
    remap_cell,
    remap_weight,
    ocean_u,
    ocean_v,
    ocean_mask,
    coriolis,
):
    f32 = jnp.float32
    components, width, _ = spectrum.shape
    levels, height, length = ocean_u.shape
    taps = remap_cell.shape[2]
    quantities = bulk_weight.shape[0]
    padded = -(-(components + PAIR) // LANES) * LANES
    coef = courant(components, NFREQ)
    cell = jnp.transpose(remap_cell, (0, 2, 1))
    weight = jnp.transpose(remap_weight, (0, 2, 1))
    messages = 2 * levels + 2 * taps
    S = jax.ShapeDtypeStruct
    dma = pltpu.SemaphoreType.DMA
    x1, ghost, cells, weights, rows_in, cols_in = pl.pallas_call(
        wave_kernel,
        name="wave_first",
        out_shape=(
            S((width + 2, components, LANES), f32),
            S((components, LANES), f32),
            S((taps, height, length), jnp.int32),
            S((taps, height, length), f32),
            S((2, messages, length), f32),
            S((2, height, LANES), f32),
        ),
        in_specs=[ANY, VMEM, ANY, ANY, ANY, ANY, ANY, ANY],
        out_specs=(ANY,) * 6,
        scratch_shapes=[
            pltpu.VMEM((width + 4, components, LANES), f32),
            pltpu.VMEM((width + 2, components, LANES), f32),
            pltpu.VMEM((components, (width + 1) * LANES), jnp.bfloat16),
            pltpu.VMEM((components, 2 * LANES), jnp.bfloat16),
            pltpu.VMEM((components, components), jnp.bfloat16),
            pltpu.VMEM((components, 8), f32),
            pltpu.VMEM((width + 4, PAIR, LANES), f32),
            pltpu.VMEM((2, width, LANES), jnp.int32),
            pltpu.VMEM((padded, LANES), f32),
            pltpu.VMEM((32, padded), f32),
            pltpu.VMEM((LANES, padded), f32),
            pltpu.VMEM((padded, LANES), f32),
            pltpu.VMEM((components, LANES), f32),
            pltpu.VMEM((height, taps, length), jnp.int32),
            pltpu.VMEM((height, taps, length), f32),
            pltpu.VMEM((levels, height, length), f32),
            pltpu.VMEM((levels, height, length), f32),
            pltpu.VMEM((taps, height, length), jnp.int32),
            pltpu.VMEM((taps, height, length), f32),
            pltpu.VMEM((2, messages, length), f32),
            pltpu.VMEM((2, height, LANES), f32),
            pltpu.VMEM((2, messages, length), f32),
            pltpu.VMEM((2, height, LANES), f32),
            dma((16,)),
            dma((24,)),
            dma((24,)),
            dma((20,)),
        ],
        compiler_params=pltpu.CompilerParams(
            collective_id=0, has_side_effects=True, vmem_limit_bytes=GRANT
        ),
    )(spectrum, sea_mask, transfer, coef, cell, weight, ocean_u, ocean_v)

    bulk_columns = jnp.pad(bulk_weight.T, ((0, 0), (0, 8 - quantities)))
    spectrum_out, bulk = pl.pallas_call(
        second_kernel,
        name="wave_second",
        out_shape=(S(spectrum.shape, f32), S((quantities, width, LANES), f32)),
        in_specs=[ANY, ANY, VMEM, ANY, ANY, ANY],
        out_specs=(ANY, VMEM),
        scratch_shapes=[
            pltpu.VMEM((width + 2, components, LANES), f32),
            pltpu.VMEM((width, components, LANES), f32),
            pltpu.VMEM((components, width * LANES), jnp.bfloat16),
            pltpu.VMEM((components, components), jnp.bfloat16),
            pltpu.VMEM((components, 8), f32),
            pltpu.VMEM((components, 8), f32),
            pltpu.VMEM((components, LANES), f32),
            dma((24,)),
            dma((24,)),
        ],
        compiler_params=pltpu.CompilerParams(vmem_limit_bytes=GRANT),
    )(x1, ghost, sea_mask, transfer, coef, bulk_columns)

    near, sides, far = pl.pallas_call(
        spread_kernel,
        name="spread",
        out_shape=(
            S((3, quantities, width, LANES), f32),
            S((2, 3, 2, width, LANES), f32),
            S((2, 2, width, LANES), f32),
        ),
        in_specs=[VMEM],
        out_specs=(VMEM,) * 3,
        scratch_shapes=[dma((12,)), dma((12,))],
        compiler_params=pltpu.CompilerParams(collective_id=1, has_side_effects=True),
    )(bulk)

    ocean_u_out, ocean_v_out = pl.pallas_call(
        ocean_kernel,
        name="ocean",
        out_shape=(S(ocean_u.shape, f32), S(ocean_v.shape, f32)),
        in_specs=[VMEM] * 11,
        out_specs=(VMEM, VMEM),
        scratch_shapes=[
            pltpu.VMEM((quantities, 8 + 3 * width + 8, LANES), f32),
            pltpu.VMEM((quantities, 9 * width, LANES), f32),
            pltpu.VMEM((2, 2, 9 * width, LANES), f32),
            pltpu.VMEM((quantities, height, length), f32),
            pltpu.VMEM((8, length), f32),
            pltpu.VMEM((8, length), f32),
            pltpu.VMEM((2, 8, length), f32),
        ],
        compiler_params=pltpu.CompilerParams(vmem_limit_bytes=GRANT),
    )(
        near, sides, far, cells, weights, rows_in, cols_in, ocean_u, ocean_v, ocean_mask,
        coriolis[None],
    )
    return (spectrum_out, ocean_u_out, ocean_v_out)


def solution(mesh):
    placed = (
        P(None, "lon", "lat"),
        P("lon", "lat"),
        P(),
        P(),
        P("lon", "lat", None),
        P("lon", "lat", None),
        P(None, "lon", "lat"),
        P(None, "lon", "lat"),
        P("lon", "lat"),
        P("lat"),
    )
    return jax.shard_map(
        local,
        mesh=mesh,
        in_specs=placed,
        out_specs=(P(None, "lon", "lat"), P(None, "lon", "lat"), P(None, "lon", "lat")),
        check_vma=False,
    )
```

time: 384 us -> 142 us (0.37); the launches traced: 379 us -> 141 us
  local copies, waits for them, and re-layouts: 220 us -> 2.98 us
  Pallas kernels: 0 us -> 137 us
  other arithmetic: 91.3 us -> 0.83 us
  starting transfers between devices: 50 us -> 0 us
  matrix products: 11.5 us -> 0 us
  waiting for transfers between devices: 5.38 us -> 0 us
    pallas_call x0 -> x4, Pallas kernels: none -> 137 us  [the longest x1 63.5 us: local(): pl.pallas_call(wave_kernel, name='wave_first', out_shape=(S((width + 2, c...]
    gather x1 -> x0, local copies, waits for them, and re-layouts: 122 us -> none  [local(): jnp.take(near, position.reshape(-1), axis=1)]
    slice x12 -> x0, local copies, waits for them, and re-layouts: 57.1 us -> none  [the longest x4 19.7 us: lat_sides(): below = passed_along(centre[:, :, -1:], 'lat', 1)]
    reduce_sum x1 -> x0, other arithmetic: 55.7 us -> none  [local(): forcing = jnp.sum(taken * remap_weight[None], axis=-1)]
    ppermute x14 -> x0, starting transfers between devices: 50 us -> none  [the longest x5 27.3 us: with_halo(): after = lax.ppermute(first, axis, down)]
    unnamed x3 -> x0, other arithmetic: 26.5 us -> none
    ppermute x4 -> x0, local copies, waits for them, and re-layouts: 15.2 us -> none  [passed_along(): lax.ppermute(value, axis, [(source, source + steps) for source in range(f...]
    unnamed x31 -> x5, local copies, waits for them, and re-layouts: 12.8 us -> 0.27 us
  transfers between devices with their start and end apart: 14 -> 0, of which waited for: 2 -> 0; matrix products, arithmetic and copies ran while one was open for 19% -> 0% of each run, Pallas kernels for 0% -> 0%
where the time goes in v2:
time: 142 us; the launch traced here: 141 us
  Pallas kernels  137 us (96%)
  local copies, waits for them, and re-layouts  2.98 us (2%)
    pallas_call x1, Pallas kernels, local(): pl.pallas_call(wave_kernel, name='wave_first', out_shape=(S((width + 2, c...  63.5 us
    pallas_call x1, Pallas kernels, local(): pl.pallas_call(second_kernel, name='wave_second', out_shape=(S(spectrum.s...  44.3 us
    pallas_call x1, Pallas kernels, local(): pl.pallas_call(spread_kernel, name='spread', out_shape=(S((3, quantities,...  16.6 us
    pallas_call x1, Pallas kernels, local(): pl.pallas_call(ocean_kernel, name='ocean', out_shape=(S(ocean_u.shape, f3...  12.5 us

profile of v2, /device:TPU:1, one launch (start us, length us, event | category | flops | bytes accessed | tf_op | source)
XLA Modules:
  0.0 141.4 jit_solution(4188700142686728468)
XLA Ops:
  0.6 0.2 negate_maximum_fusion
  0.8 0.2 subtract_subtract_fusion
  1.1 0.2 broadcast_maximum_fusion.1
  1.3 0.2 fusion.8
  1.5 0.1 stack.2
  1.6 1.1 copy.14.coef_hbm
  2.7 0.0 copy-start
  2.7 63.5 %wave_first.1 = (f32[10,1296,128]{2,1,0:T(8,128)}, f32[1296,128]{1,0:T(8,128)}, s32[4,24,384]{2,1,0:T(8,128)}, f32[4,24,384]{2,1,0:T(8,128)}, f32[2,24,384]{2,1,0:T(8,128)}, /*index=5*/f32[2,24,128]{2,1,0:T(8,128)}) custom-call(f32[1296,8,128]{2,1,0:T(8,128)} %spectrum.1, s32[8,128]{1,0:T(8,128)} %sea.4, bf16[1296,1296]{1,0:T(8,128)(2,1)} %transfer.3, ...), custom_call_target="tpu_custom_call" | custom-call | tf_op jit(solution)/shard_map/wave_first/pallas_call | solution.py:851
  66.2 0.0 copy-done
  66.2 0.3 copy.15
  66.4 1.0 pad.4.bulk_hbm
  67.4 0.0 copy-start.1
  67.4 44.3 %wave_second.1 = (f32[1296,8,128]{2,1,0:T(8,128)}, f32[5,8,128]{2,1,0:T(8,128)}) custom-call(f32[10,1296,128]{2,1,0:T(8,128)} %get-tuple-element.16.x1_hbm, f32[1296,128]{1,0:T(8,128)} %get-tuple-element.17.ghost_hbm, s32[8,128]{1,0:T(8,128)} %sea.4, bf16[1296,1296]{1,0:T(8,128)(2,1)} %transfer.3, f32[1296,8]{1,0:T(8,128)} %copy.14.coef_hbm, ...), custom_call_target="tpu_custom_call" | custom-call | tf_op jit(solution)/shard_map/wave_second/pallas_call | solution.py:899
  111.7 16.6 %spread.1 = (f32[3,5,8,128]{3,2,1,0:T(8,128)}, f32[2,3,2,8,128]{4,3,2,1,0:T(8,128)}, f32[2,2,8,128]{3,2,1,0:T(8,128)}) custom-call(f32[5,8,128]{2,1,0:T(8,128)} %get-tuple-element.19.bulk), custom_call_target="tpu_custom_call" | custom-call | tf_op jit(solution)/shard_map/spread/pallas_call | solution.py:919
  128.3 0.0 copy-done.1
  128.3 0.6 broadcast_in_dim.3.coriolis
  128.9 12.5 %ocean.1 = (f32[8,24,384]{2,1,0:T(8,128)}, f32[8,24,384]{2,1,0:T(8,128)}) custom-call(f32[3,5,8,128]{3,2,1,0:T(8,128)} %get-tuple-element.20.near, f32[2,3,2,8,128]{4,3,2,1,0:T(8,128)} %get-tuple-element.21.sides, f32[2,2,8,128]{3,2,1,0:T(8,128)} %get-tuple-element.22.far, s32[4,24,384]{2,1,0:T(8,128)} %get-tuple-element.23.cells, ...), custom_call_target="tpu_custom_call" | custom-call | tf_op jit(solution)/shard_map/ocean/pallas_call | solution.py:933
  (1 shorter events, 0.0 us)
Async XLA Ops:
  2.7 63.5 %copy-start = (f32[5,1296]{1,0:T(8,128)S(1)}, f32[5,1296]{1,0:T(8,128)}, u32[]{:S(2)}) copy-start(f32[5,1296]{1,0:T(8,128)} %param.13) | copy-start | bytes 77764
  67.4 61.0 %copy-start.1 = (f32[384]{0:T(512)S(1)}, f32[384]{0:T(512)}, u32[]{:S(2)}) copy-start(f32[384]{0:T(512)} %param.19) | copy-start | bytes 4612

commit v3 on v2

v3 whole, which is shorter than its diff:
```python
import math

import jax
import jax.numpy as jnp
import numpy as np
from jax import lax
from jax.experimental import pallas as pl
from jax.experimental.pallas import tpu as pltpu
from jax.sharding import PartitionSpec as P

NFREQ = 36
MESH = pl.DeviceIdType.MESH
VMEM = pl.BlockSpec(memory_space=pltpu.VMEM)
ANY = pl.BlockSpec(memory_space=pl.ANY)
LANES = 128
PAIR = 16
GRANT = 60 * 1024 * 1024


def courant(components, freqs):
    index = np.arange(components)
    theta = 2.0 * np.pi * (index // freqs + 0.5) / (components // freqs)
    speed = 1.1 ** -(index % freqs).astype(np.float64)
    east, north = 0.45 * speed * np.cos(theta), 0.45 * speed * np.sin(theta)
    parts = [1.0 - abs(east) - abs(north), abs(east), abs(north)]
    parts += [np.maximum(p, 0.0) for p in (east, -east, north, -north)] + [0.0 * east]
    return np.stack(parts, axis=1).astype(np.float32)


def sign_of(function, first, last, freqs, directions):
    signs = set()
    for d in range(first // freqs, (last - 1) // freqs + 1):
        signs.add(1 if function(2 * math.pi * (d + 0.5) / directions) > 0 else -1)
    return signs.pop() if len(signs) == 1 else 0


def segments(components, freqs):
    directions = components // freqs
    runs = []
    for pair in range(components // PAIR):
        first, last = pair * PAIR, (pair + 1) * PAIR
        key = (
            sign_of(math.cos, first, last, freqs, directions),
            sign_of(math.sin, first, last, freqs, directions),
        )
        if runs and runs[-1][2] == key:
            runs[-1][1] = pair + 1
        else:
            runs.append([pair, pair + 1, key])
    return [(a, b, xs, ys) for a, b, (xs, ys) in runs]


def row_spans(components, freqs, sign):
    spans = []
    for a, b, xs, _ in segments(components, freqs):
        if xs == -sign:
            continue
        if spans and spans[-1][1] == a * PAIR:
            spans[-1][1] = b * PAIR
        else:
            spans.append([a * PAIR, b * PAIR])
    return [tuple(s) for s in spans]


def complement(spans, total):
    out, at = [], 0
    for a, b in spans:
        if a > at:
            out.append((at, a))
        at = b
    if at < total:
        out.append((at, total))
    return out


def south_lane(c):
    return 2 * c + 1 if 0 <= c < 8 else (32 if c < 0 else 33)


def north_lane(c):
    return 16 + 2 * c if 0 <= c < 8 else (34 if c < 0 else 35)


def lane_shift(x, source, target):
    return pltpu.roll(x, (target - source) % LANES, 1)


def coefficients(coef, wide, r, xs, ys):
    rows = pl.ds(r, PAIR)

    def spread(n):
        return jnp.broadcast_to(coef[rows, n : n + 1], (PAIR, LANES))

    return dict(
        c=wide[0, rows, :],
        x=wide[1, rows, :] if xs else (spread(3), spread(4)),
        y=wide[2, rows, :] if ys else (spread(5), spread(6)),
    )


def upwind(co, xs, ys, centre, west, east, south, north):
    result = co["c"] * centre
    if xs:
        result = result + co["x"] * (west() if xs > 0 else east())
    else:
        result = result + co["x"][0] * west() + co["x"][1] * east()
    if ys:
        result = result + co["y"] * (south() if ys > 0 else north())
    else:
        result = result + co["y"][0] * south() + co["y"][1] * north()
    return result


def advect_columns(co, xs, ys, columns, state, ghost, lane):
    out = {}
    for c in columns:
        out[c] = upwind(
            co,
            xs,
            ys,
            state[c],
            lambda: state[c - 1],
            lambda: state[c + 1],
            lambda: jnp.where(
                lane == 0, lane_shift(ghost, south_lane(c), 0), pltpu.roll(state[c], 1, 1)
            ),
            lambda: jnp.where(
                lane == LANES - 1,
                lane_shift(ghost, north_lane(c), LANES - 1),
                pltpu.roll(state[c], LANES - 1, 1),
            ),
        )
    return out


def needed(columns, xs):
    want = set(columns)
    if xs >= 0:
        want |= {c - 1 for c in columns}
    if xs <= 0:
        want |= {c + 1 for c in columns}
    return sorted(want)


def over_rows(runs, body, unroll=10):
    for a, b, xs, ys in runs:
        steps = (b - a) // unroll
        if steps > 1:

            def step(p, carry, a=a, xs=xs, ys=ys):
                for j in range(unroll):
                    body(pl.multiple_of((a + p * unroll + j) * PAIR, PAIR), xs, ys)
                return carry

            lax.fori_loop(0, steps, step, 0)
            a += steps * unroll
        for p in range(a, b):
            body(p * PAIR, xs, ys)


def repeat(count, body, unroll):
    def step(p, carry):
        for j in range(unroll):
            body(p * unroll + j)
        return carry

    lax.fori_loop(0, count // unroll, step, 0)
    for p in range(count // unroll * unroll, count):
        body(p)


def bulk_of(bulk_wide, state, columns, quantities, components, bulk):
    unroll = 9

    def gather(p, totals):
        totals = list(totals)
        for j in range(unroll):
            rows = pl.ds(pl.multiple_of((p * unroll + j) * 8, 8), 8)
            wide = [bulk_wide[q, rows, :] for q in range(quantities)]
            for n, c in enumerate(columns):
                value = state[c + 2, rows, :]
                for q in range(quantities):
                    at = n * quantities + q
                    totals[at] = totals[at] + wide[q] * value
        return tuple(totals)

    zero = jnp.zeros((8, LANES), jnp.float32)
    totals = lax.fori_loop(
        0, components // 8 // unroll, gather, (zero,) * (len(columns) * quantities)
    )
    for n, c in enumerate(columns):
        for q in range(quantities):
            bulk[q, pl.ds(c, 1), :] = jnp.sum(
                totals[n * quantities + q], axis=0, keepdims=True
            )


def wave_kernel(
    spectrum, sea, transfer, coef_hbm, bulk_weight, cell_hbm, weight_hbm, u_hbm, v_hbm,
    s2_out, near_out, sides_out, far_out, cells_out, weights_out, rows_out, cols_out,
    x, a, ab, abe, t, coef, wide, bulk_turned, bulk_wide, masks, packed, turned, gturned, g, ga,
    cell, weight, u, v, cells, weights, rows_send, cols_send, rows_in, cols_in,
    bulk, near, sides, far, far_masks, local_sem, send_sem, recv_sem, out_sem,
):
    lon, lat = lax.axis_index("lon"), lax.axis_index("lat")
    nlon, nlat = lax.axis_size("lon"), lax.axis_size("lat")
    components, width, _ = spectrum.shape
    quantities = bulk_weight.shape[0]
    runs = segments(components, NFREQ)
    plus = row_spans(components, NFREQ, 1)
    minus = row_spans(components, NFREQ, -1)
    around = [lax.rem(lon + d + nlon, nlon) for d in (-2, -1, 0, 1, 2)]
    east, west = around[3], around[1]
    has_south, has_north = lat > 0, lat < nlat - 1
    lane = lax.broadcasted_iota(jnp.int32, (PAIR, LANES), 1)

    gturned[...] = jnp.zeros_like(gturned)
    cols_in[...] = jnp.zeros_like(cols_in)
    sides[...] = jnp.zeros_like(sides)

    local = []

    def load(src, dst):
        copy = pltpu.make_async_copy(src, dst, local_sem.at[len(local)])
        copy.start()
        local.append(copy)
        return copy

    barrier = pltpu.get_barrier_semaphore()

    def greet(to_lon, to_lat):
        pl.semaphore_signal(barrier, inc=1, device_id=(to_lon, to_lat), device_id_type=MESH)

    for d in (0, 1, 3, 4):
        greet(around[d], lat)

    @pl.when(has_north)
    def _():
        for d in (1, 2, 3):
            greet(around[d], lat + 1)

    @pl.when(has_south)
    def _():
        for d in (1, 2, 3):
            greet(around[d], lat - 1)

    columns_in = [load(spectrum.at[:, c, :], x.at[c + 2]) for c in range(width)]
    coef_in = load(coef_hbm, coef)
    cell_in = load(cell_hbm, cell)
    weight_in = load(weight_hbm, weight)
    u_in = load(u_hbm, u)
    v_in = load(v_hbm, v)
    transfer_in = load(transfer, t)

    pl.semaphore_wait(
        barrier, 4 + 3 * has_north.astype(jnp.int32) + 3 * has_south.astype(jnp.int32)
    )

    count = [0]

    def remote(src, dst, to_lon, to_lat):
        n = count[0]
        count[0] += 1
        return pltpu.make_async_remote_copy(
            src_ref=src,
            dst_ref=dst,
            send_sem=send_sem.at[n],
            recv_sem=recv_sem.at[n],
            device_id=(to_lon, to_lat),
            device_id_type=MESH,
        )

    def columns(spans, source, target, to_lon):
        return [
            remote(source(pl.ds(k0, k1 - k0)), target(pl.ds(k0, k1 - k0)), to_lon, lat)
            for k0, k1 in spans
        ]

    first = columns(
        plus, lambda k: spectrum.at[k, width - 1, :], lambda k: x.at[1, k, :], east
    ) + columns(minus, lambda k: spectrum.at[k, 0, :], lambda k: x.at[width + 2, k, :], west)
    second = columns(
        plus, lambda k: a.at[width, k, :], lambda k: a.at[0, k, :], east
    ) + columns(minus, lambda k: a.at[1, k, :], lambda k: a.at[width + 1, k, :], west)
    side_masks = [
        remote(sea.at[pl.ds(width - 1, 1), :], far_masks.at[0], east, lat),
        remote(sea.at[pl.ds(0, 1), :], far_masks.at[1], west, lat),
    ]
    for copy in side_masks + first:
        copy.start()

    for c in range(width):
        masks[c + 2] = jnp.broadcast_to(
            sea[pl.ds(c, 1), :].astype(jnp.float32), (PAIR, LANES)
        )

    for copy in columns_in:
        copy.wait()

    def pack(r, values):
        total = jnp.zeros((PAIR, LANES), jnp.float32)
        half = lane // 2
        for c in range(width):
            total = jnp.where(half == c, lane_shift(values[c], LANES - 2, 2 * c), total)
            total = jnp.where(half == 8 + c, lane_shift(values[c], 0, 16 + 2 * c), total)
        packed[pl.ds(r, PAIR), :] = total

    def pack_rows(p):
        r = pl.multiple_of(p * PAIR, PAIR)
        values = []
        for c in range(width):
            value = x[c + 2, pl.ds(r, PAIR), :] * masks[c + 2]
            x[c + 2, pl.ds(r, PAIR), :] = value
            values.append(value)
        pack(r, values)

    repeat(components // PAIR, pack_rows, 9)
    pack(components, [masks[c + 2] for c in range(width)])
    blocks = packed.shape[0] // LANES
    tail = components + PAIR
    packed[pl.ds(tail, blocks * LANES - tail), :] = jnp.zeros(
        (blocks * LANES - tail, LANES), jnp.float32
    )
    for b in range(blocks):
        turned[:, b * LANES : (b + 1) * LANES] = jnp.transpose(
            packed[b * LANES : (b + 1) * LANES, :]
        )[:32, :]

    to_north = [
        remote(turned.at[pl.ds(0, 16), :], gturned.at[pl.ds(0, 16), :], lon, lat + 1),
        remote(turned.at[pl.ds(15, 1), :], gturned.at[pl.ds(32, 1), :], east, lat + 1),
        remote(turned.at[pl.ds(1, 1), :], gturned.at[pl.ds(33, 1), :], west, lat + 1),
    ]
    to_south = [
        remote(turned.at[pl.ds(16, 16), :], gturned.at[pl.ds(16, 16), :], lon, lat - 1),
        remote(turned.at[pl.ds(30, 1), :], gturned.at[pl.ds(34, 1), :], east, lat - 1),
        remote(turned.at[pl.ds(16, 1), :], gturned.at[pl.ds(35, 1), :], west, lat - 1),
    ]

    @pl.when(has_north)
    def _():
        for copy in to_north:
            copy.start()

    @pl.when(has_south)
    def _():
        for copy in to_south:
            copy.start()

    coef_in.wait()
    bulk_turned[...] = jnp.zeros_like(bulk_turned)
    for b in range(blocks):
        low = b * LANES
        high = min(low + LANES, components)
        bulk_turned[pl.ds(0, quantities), : high - low] = bulk_weight[:, low:high]
        part = jnp.transpose(bulk_turned[...])
        rows = pl.ds(low, high - low)
        for q in range(quantities):
            bulk_wide[q, rows, :] = jnp.broadcast_to(
                part[: high - low, q : q + 1], (high - low, LANES)
            )

    def widen(p):
        rows = pl.ds(pl.multiple_of(p * PAIR, PAIR), PAIR)
        line = coef[rows, :]
        for n in range(3):
            wide[n, rows, :] = jnp.broadcast_to(line[:, n : n + 1], (PAIR, LANES))

    repeat(components // PAIR, widen, 9)

    for copy in (cell_in, weight_in, u_in, v_in):
        copy.wait()
    height, taps, length = cell.shape
    for i in range(height):
        for tap in range(taps):
            cells[tap, pl.ds(i, 1), :] = cell[i, pl.ds(tap, 1), :]
            weights[tap, pl.ds(i, 1), :] = weight[i, pl.ds(tap, 1), :]
    levels = u.shape[0]
    for side, row in ((0, height - 1), (1, 0)):
        for level in range(levels):
            rows_send[side, pl.ds(level, 1), :] = u[level, pl.ds(row, 1), :]
            rows_send[side, pl.ds(levels + level, 1), :] = v[level, pl.ds(row, 1), :]
        for tap in range(taps):
            rows_send[side, pl.ds(2 * levels + tap, 1), :] = weights[tap, pl.ds(row, 1), :]
            rows_send[side, pl.ds(2 * levels + taps + tap, 1), :] = cells[
                tap, pl.ds(row, 1), :
            ].astype(jnp.float32)
    lane_all = lax.broadcasted_iota(jnp.int32, (height, LANES), 1)
    for side, start, source in ((0, length - LANES, LANES - 1), (1, 0, 0)):
        total = jnp.zeros((height, LANES), jnp.float32)
        for n in range(2 * levels + 2 * taps):
            if n < levels:
                block = u[n, :, start : start + LANES]
            elif n < 2 * levels:
                block = v[n - levels, :, start : start + LANES]
            elif n < 2 * levels + taps:
                block = weights[n - 2 * levels, :, start : start + LANES]
            else:
                block = cells[n - 2 * levels - taps, :, start : start + LANES].astype(jnp.float32)
            total = jnp.where(lane_all == n, lane_shift(block, source, n), total)
        cols_send[side] = total

    stores = []

    def store(src, dst):
        copy = pltpu.make_async_copy(src, dst, out_sem.at[len(stores)])
        copy.start()
        stores.append(copy)

    store(cells, cells_out)
    store(weights, weights_out)

    @pl.when(has_south)
    def _():
        for copy in to_north:
            copy.wait_recv()

    @pl.when(has_north)
    def _():
        for copy in to_south:
            copy.wait_recv()

    for b in range(blocks):
        g[b * LANES : (b + 1) * LANES, :] = jnp.transpose(
            gturned[:, b * LANES : (b + 1) * LANES]
        )
    inner = list(range(1, width - 1))
    outer = [0, width - 1]
    ghost_at = len(inner) * LANES

    def first_inner(r, xs, ys):
        co = coefficients(coef, wide, r, xs, ys)
        rows = pl.ds(r, PAIR)
        state = {c: x[c + 2, rows, :] for c in needed(inner, xs)}
        ghost = g[rows, :]
        mine = packed[rows, :]
        for c, value in advect_columns(co, xs, ys, inner, state, ghost, lane).items():
            a[c + 1, rows, :] = value
            ab[rows, (c - 1) * LANES : c * LANES] = value.astype(jnp.bfloat16)

        def sideways(step, low, high):
            moved = pltpu.roll(ghost, step % LANES, 1)
            for target, source in (low, high):
                moved = jnp.where(lane == target, lane_shift(ghost, source, target), moved)
            return moved

        value = upwind(
            co,
            xs,
            ys,
            ghost,
            lambda: sideways(2, (1, 32), (16, 34)),
            lambda: sideways(-2, (15, 33), (30, 35)),
            lambda: jnp.where(lane < 16, pltpu.roll(ghost, 1, 1), pltpu.roll(mine, 15, 1)),
            lambda: jnp.where(
                lane < 16, pltpu.roll(mine, LANES - 15, 1), pltpu.roll(ghost, LANES - 1, 1)
            ),
        )
        ga[rows, :] = value
        ab[rows, ghost_at : ghost_at + LANES] = value.astype(jnp.bfloat16)

    over_rows(runs, first_inner)
    transfer_in.wait()
    block = 432
    ghost_mask = g[pl.ds(components, 1), :]

    def inner_product(state, shift, with_ghost):
        def product(m, carry):
            rows = pl.ds(pl.multiple_of(m * block, PAIR), block)
            for n in range(0, len(inner), 2):
                added = jnp.dot(
                    t[rows, :],
                    ab[:, n * LANES : (n + 2) * LANES],
                    preferred_element_type=jnp.float32,
                )
                for c in (n + 1, n + 2):
                    part = added[:, (c - n - 1) * LANES : (c - n) * LANES]
                    state[c + shift, rows, :] = masks[c + 2, pl.ds(0, 1), :] * (
                        state[c + shift, rows, :] + 0.5 * part
                    )
            if with_ghost:
                added = jnp.dot(
                    t[rows, :],
                    ab[:, ghost_at : ghost_at + LANES],
                    preferred_element_type=jnp.float32,
                )
                ga[rows, :] = ghost_mask * (ga[rows, :] + 0.5 * added)
            return carry

        lax.fori_loop(0, components // block, product, 0)

    def outer_product(state, shift):
        def product(m, carry):
            rows = pl.ds(pl.multiple_of(m * block, PAIR), block)
            added = jnp.dot(t[rows, :], abe[...], preferred_element_type=jnp.float32)
            for n, c in enumerate(outer):
                part = added[:, n * LANES : (n + 1) * LANES]
                state[c + shift, rows, :] = masks[c + 2, pl.ds(0, 1), :] * (
                    state[c + shift, rows, :] + 0.5 * part
                )
            return carry

        lax.fori_loop(0, components // block, product, 0)

    inner_product(a, 1, True)

    for copy in side_masks + first:
        copy.wait_recv()
    rows_copy = [
        remote(rows_send.at[0], rows_in.at[0], east, lat),
        remote(rows_send.at[1], rows_in.at[1], west, lat),
    ]
    cols_north = remote(cols_send.at[0], cols_in.at[0], lon, lat + 1)
    cols_south = remote(cols_send.at[1], cols_in.at[1], lon, lat - 1)
    for copy in rows_copy:
        copy.start()

    @pl.when(has_north)
    def _():
        cols_north.start()

    @pl.when(has_south)
    def _():
        cols_south.start()

    for slot, side in ((1, 0), (width + 2, 1)):
        masks[slot] = jnp.broadcast_to(far_masks[side].astype(jnp.float32), (PAIR, LANES))

    def first_outer(r, xs, ys):
        co = coefficients(coef, wide, r, xs, ys)
        rows = pl.ds(r, PAIR)
        state = {}
        for c in needed(outer, xs):
            value = x[c + 2, rows, :]
            state[c] = value * masks[c + 2] if c in (-1, width) else value
        for n, (c, value) in enumerate(
            advect_columns(co, xs, ys, outer, state, g[rows, :], lane).items()
        ):
            a[c + 1, rows, :] = value
            abe[rows, n * LANES : (n + 1) * LANES] = value.astype(jnp.bfloat16)

    over_rows(runs, first_outer)
    outer_product(a, 1)
    for copy in second:
        copy.start()

    def second_step(group, target):
        def step(r, xs, ys):
            co = coefficients(coef, wide, r, xs, ys)
            rows = pl.ds(r, PAIR)
            state = {c: a[c + 1, rows, :] for c in needed(group, xs)}
            for n, (c, value) in enumerate(
                advect_columns(co, xs, ys, group, state, ga[rows, :], lane).items()
            ):
                x[c + 2, rows, :] = value
                target[rows, n * LANES : (n + 1) * LANES] = value.astype(jnp.bfloat16)

        over_rows(runs, step)

    for copy in side_masks + first:
        copy.wait_send()
    second_step(inner, ab)
    inner_product(x, 2, False)
    for c in inner:
        store(x.at[c + 2], s2_out.at[c])
    bulk_of(bulk_wide, x, inner, quantities, components, bulk)

    for copy in second:
        copy.wait_recv()
    second_step(outer, abe)
    outer_product(x, 2)
    for c in outer:
        store(x.at[c + 2], s2_out.at[c])
    bulk_of(bulk_wide, x, outer, quantities, components, bulk)

    drift = bulk.at[pl.ds(1, 2)]
    stress = bulk.at[pl.ds(0, 2)]
    flat = [
        remote(bulk, near.at[2], west, lat),
        remote(bulk, near.at[0], east, lat),
        remote(stress, far.at[1], around[0], lat),
        remote(stress, far.at[0], around[4], lat),
    ]
    spread_north = [
        remote(drift, sides.at[0, 2], west, lat + 1),
        remote(drift, sides.at[0, 1], lon, lat + 1),
        remote(drift, sides.at[0, 0], east, lat + 1),
    ]
    spread_south = [
        remote(drift, sides.at[1, 2], west, lat - 1),
        remote(drift, sides.at[1, 1], lon, lat - 1),
        remote(drift, sides.at[1, 0], east, lat - 1),
    ]
    for copy in flat:
        copy.start()

    @pl.when(has_north)
    def _():
        for copy in spread_north:
            copy.start()

    @pl.when(has_south)
    def _():
        for copy in spread_south:
            copy.start()

    near[1] = bulk[...]

    for copy in rows_copy:
        copy.wait()
    for copy in second:
        copy.wait_send()

    @pl.when(has_north)
    def _():
        for copy in to_north + [cols_north]:
            copy.wait_send()
        cols_south.wait_recv()

    @pl.when(has_south)
    def _():
        for copy in to_south + [cols_south]:
            copy.wait_send()
        cols_north.wait_recv()

    store(rows_in, rows_out)
    store(cols_in, cols_out)

    for copy in flat:
        copy.wait()

    @pl.when(has_north)
    def _():
        for copy in spread_north:
            copy.wait_send()
        for copy in spread_south:
            copy.wait_recv()

    @pl.when(has_south)
    def _():
        for copy in spread_south:
            copy.wait_send()
        for copy in spread_north:
            copy.wait_recv()

    store(near, near_out)
    store(sides, sides_out)
    store(far, far_out)
    for copy in stores:
        copy.wait()


def taken_from(sources, codes, quantities):
    places = [c & (LANES - 1) for c in codes]
    offsets = [c >> 9 for c in codes]
    taken = [[jnp.zeros(codes[0].shape, jnp.float32)] * len(quantities) for _ in codes]
    for o in range(17):
        hits = [offset == o for offset in offsets]
        for n, q in enumerate(quantities):
            source = sources(q, o)
            for i in range(len(codes)):
                got = jnp.take_along_axis(source, places[i], axis=1, mode="promise_in_bounds")
                taken[i][n] = jnp.where(hits[i], got, taken[i][n])
    return taken


def ocean_kernel(
    s2, near, sides, far, cells, weights, rows_in, cols_in, u, v, sea, coriolis,
    spectrum_out, u_out, v_out,
    near1, near3, sides3, forcing, edge_code, edge_weight, edge_rows, state, in_sem, out_sem,
):
    quantities = near.shape[1]
    width = near.shape[2]
    taps, height, length = cells.shape
    levels = u.shape[0]
    reads = [pltpu.make_async_copy(s2.at[c], state.at[c], in_sem.at[c]) for c in range(width)]
    writes = [
        pltpu.make_async_copy(state.at[c], spectrum_out.at[:, c, :], out_sem.at[c])
        for c in range(width)
    ]
    for copy in reads:
        copy.start()
    for part in range(3):
        near1[:, pl.ds(8 + part * width, width), :] = near[part]
    near1[pl.ds(0, 2), pl.ds(7, 1), :] = far[0, :, pl.ds(width - 1, 1), :]
    near1[pl.ds(0, 2), pl.ds(8 + 3 * width, 1), :] = far[1, :, pl.ds(0, 1), :]
    for i in range(3 * width):
        for q in range(quantities):
            near3[q, pl.ds(3 * i, 3), :] = jnp.broadcast_to(
                near1[q, pl.ds(8 + i, 1), :], (3, LANES)
            )
        for side in range(2):
            for q in range(2):
                sides3[side, q, pl.ds(3 * i, 3), :] = jnp.broadcast_to(
                    sides[side, i // width, q, pl.ds(i % width, 1), :], (3, LANES)
                )

    def block(jb, carry):
        lanes = pl.ds(pl.multiple_of(jb * LANES, LANES), LANES)
        for i0 in range(0, height, 8):
            rows = pl.ds(i0, 8)
            taken = taken_from(
                lambda q, o: near3[q, pl.ds(i0 + 3 * o, 8), :],
                [cells[tap, rows, lanes] for tap in range(taps)],
                range(quantities),
            )
            for q in range(quantities):
                total = 0.0
                for tap in range(taps):
                    total = total + taken[tap][q] * weights[tap, rows, lanes]
                forcing[q, rows, lanes] = total
        low = lax.broadcasted_iota(jnp.int32, (8, LANES), 0) < 4
        taken = taken_from(
            lambda q, o: jnp.where(
                low,
                jnp.broadcast_to(near1[q, pl.ds(7 + o, 1), :], (8, LANES)),
                jnp.broadcast_to(near1[q, pl.ds(16 + o, 1), :], (8, LANES)),
            ),
            [edge_code[:, lanes].astype(jnp.int32)],
            range(2),
        )
        for q in range(2):
            product = taken[0][q] * edge_weight[:, lanes]
            zero = jnp.zeros_like(product)
            edge_rows[q, pl.ds(0, 1), lanes] = jnp.sum(
                jnp.where(low, product, zero), axis=0, keepdims=True
            )
            edge_rows[q, pl.ds(1, 1), lanes] = jnp.sum(
                jnp.where(low, zero, product), axis=0, keepdims=True
            )
        return carry

    for read, write in zip(reads, writes):
        read.wait()
        write.start()
    for side in range(2):
        edge_code[pl.ds(4 * side, 4), :] = rows_in[side, pl.ds(2 * levels + taps, taps), :]
        edge_weight[pl.ds(4 * side, 4), :] = rows_in[side, pl.ds(2 * levels, taps), :]
    lax.fori_loop(0, length // LANES, block, 0)

    lane = lax.broadcasted_iota(jnp.int32, (8, LANES), 1)
    here = jnp.logical_and(lane >= 2 * levels + taps, lane < 2 * levels + 2 * taps)
    edge_cols = [[], []]
    for side in range(2):
        parts = [[], []]
        for i0 in range(0, height, 8):
            line = cols_in[side, pl.ds(i0, 8), :]
            code = jnp.where(here, line, 0.0).astype(jnp.int32)
            taken = taken_from(
                lambda q, o: sides3[side, q, pl.ds(i0 + 3 * o, 8), :], [code], range(2)
            )
            weight = jnp.where(here, pltpu.roll(line, taps, 1), 0.0)
            for q in range(2):
                parts[q].append(jnp.sum(taken[0][q] * weight, axis=1, keepdims=True))
        for q in range(2):
            edge_cols[side].append(jnp.concatenate(parts[q], axis=0))

    row = lax.broadcasted_iota(jnp.int32, (height, length), 0)
    col = lax.broadcasted_iota(jnp.int32, (height, length), 1)

    def shifted(q, west, east, south, north):
        return (
            jnp.where(row == 0, west, pltpu.roll(q, 1, 0)),
            jnp.where(row == height - 1, east, pltpu.roll(q, height - 1, 0)),
            jnp.where(col == 0, south, pltpu.roll(q, 1, 1)),
            jnp.where(col == length - 1, north, pltpu.roll(q, length - 1, 1)),
        )

    def dx(q, index):
        low = jnp.where(row == 0, edge_rows[index, pl.ds(0, 1), :], pltpu.roll(q, 1, 0))
        high = jnp.where(
            row == height - 1, edge_rows[index, pl.ds(1, 1), :], pltpu.roll(q, height - 1, 0)
        )
        return 0.5 * (high - low)

    def dy(q, index):
        low = jnp.where(col == 0, edge_cols[0][index], pltpu.roll(q, 1, 1))
        high = jnp.where(col == length - 1, edge_cols[1][index], pltpu.roll(q, length - 1, 1))
        return 0.5 * (high - low)

    sxx, sxy, syy = forcing[0], forcing[1], forcing[2]
    force_x = -(dx(sxx, 0) + dy(sxy, 0))
    force_y = -(dx(sxy, 1) + dy(syy, 1))
    wet = sea[...].astype(jnp.float32)
    turn = jnp.broadcast_to(0.5 * coriolis[...][None], (height, length))
    for level in range(levels):
        decay = math.exp(-level / 3.0)
        here_u, here_v = u[level], v[level]

        def laplace(q, n):
            west, east, south, north = shifted(
                q,
                rows_in[0, pl.ds(n, 1), :],
                rows_in[1, pl.ds(n, 1), :],
                cols_in[0, :, n : n + 1],
                cols_in[1, :, n : n + 1],
            )
            return east + west + north + south - 4.0 * q

        u_out[level] = wet * (
            here_u
            + turn * (here_v + decay * forcing[4])
            + (0.5 * decay) * force_x
            + 0.1 * laplace(here_u, level)
        )
        v_out[level] = wet * (
            here_v
            - turn * (here_u + decay * forcing[3])
            + (0.5 * decay) * force_y
            + 0.1 * laplace(here_v, levels + level)
        )
    for copy in writes:
        copy.wait()


def local(
    spectrum,
    sea_mask,
    transfer,
    bulk_weight,
    remap_cell,
    remap_weight,
    ocean_u,
    ocean_v,
    ocean_mask,
    coriolis,
):
    f32, i32 = jnp.float32, jnp.int32
    components, width, _ = spectrum.shape
    levels, height, length = ocean_u.shape
    taps = remap_cell.shape[2]
    quantities = bulk_weight.shape[0]
    padded = -(-(components + PAIR) // LANES) * LANES
    coef = courant(components, NFREQ)
    cell = jnp.transpose(remap_cell, (0, 2, 1))
    weight = jnp.transpose(remap_weight, (0, 2, 1))
    messages = 2 * levels + 2 * taps
    S = jax.ShapeDtypeStruct
    dma = pltpu.SemaphoreType.DMA
    near_shape = (3, quantities, width, LANES)
    sides_shape = (2, 3, 2, width, LANES)
    far_shape = (2, 2, width, LANES)
    s2, near, sides, far, cells, weights, rows_in, cols_in = pl.pallas_call(
        wave_kernel,
        name="wave",
        out_shape=(
            S((width, components, LANES), f32),
            S(near_shape, f32),
            S(sides_shape, f32),
            S(far_shape, f32),
            S((taps, height, length), i32),
            S((taps, height, length), f32),
            S((2, messages, length), f32),
            S((2, height, LANES), f32),
        ),
        in_specs=[ANY, VMEM, ANY, ANY, VMEM, ANY, ANY, ANY, ANY],
        out_specs=(ANY,) * 8,
        scratch_shapes=[
            pltpu.VMEM((width + 4, components, LANES), f32),
            pltpu.VMEM((width + 2, components, LANES), f32),
            pltpu.VMEM((components, (width - 1) * LANES), jnp.bfloat16),
            pltpu.VMEM((components, 2 * LANES), jnp.bfloat16),
            pltpu.VMEM((components, components), jnp.bfloat16),
            pltpu.VMEM((components, 8), f32),
            pltpu.VMEM((3, components, LANES), f32),
            pltpu.VMEM((LANES, LANES), f32),
            pltpu.VMEM((quantities, components, LANES), f32),
            pltpu.VMEM((width + 4, PAIR, LANES), f32),
            pltpu.VMEM((padded, LANES), f32),
            pltpu.VMEM((32, padded), f32),
            pltpu.VMEM((LANES, padded), f32),
            pltpu.VMEM((padded, LANES), f32),
            pltpu.VMEM((components, LANES), f32),
            pltpu.VMEM((height, taps, length), i32),
            pltpu.VMEM((height, taps, length), f32),
            pltpu.VMEM((levels, height, length), f32),
            pltpu.VMEM((levels, height, length), f32),
            pltpu.VMEM((taps, height, length), i32),
            pltpu.VMEM((taps, height, length), f32),
            pltpu.VMEM((2, messages, length), f32),
            pltpu.VMEM((2, height, LANES), f32),
            pltpu.VMEM((2, messages, length), f32),
            pltpu.VMEM((2, height, LANES), f32),
            pltpu.VMEM((quantities, width, LANES), f32),
            pltpu.VMEM(near_shape, f32),
            pltpu.VMEM(sides_shape, f32),
            pltpu.VMEM(far_shape, f32),
            pltpu.VMEM((2, 1, LANES), i32),
            dma((16,)),
            dma((32,)),
            dma((32,)),
            dma((16,)),
        ],
        compiler_params=pltpu.CompilerParams(
            collective_id=0, has_side_effects=True, vmem_limit_bytes=GRANT
        ),
    )(
        spectrum, sea_mask, transfer, jnp.asarray(coef), bulk_weight, cell, weight,
        ocean_u, ocean_v,
    )

    return pl.pallas_call(
        ocean_kernel,
        name="ocean",
        out_shape=(S(spectrum.shape, f32), S(ocean_u.shape, f32), S(ocean_v.shape, f32)),
        in_specs=[ANY] + [VMEM] * 11,
        out_specs=(ANY, VMEM, VMEM),
        scratch_shapes=[
            pltpu.VMEM((quantities, 8 + 3 * width + 8, LANES), f32),
            pltpu.VMEM((quantities, 9 * width, LANES), f32),
            pltpu.VMEM((2, 2, 9 * width, LANES), f32),
            pltpu.VMEM((quantities, height, length), f32),
            pltpu.VMEM((8, length), f32),
            pltpu.VMEM((8, length), f32),
            pltpu.VMEM((2, 8, length), f32),
            pltpu.VMEM((width, components, LANES), f32),
            dma((width,)),
            dma((width,)),
        ],
        compiler_params=pltpu.CompilerParams(vmem_limit_bytes=GRANT),
    )(
        s2, near, sides, far, cells, weights, rows_in, cols_in, ocean_u, ocean_v, ocean_mask,
        coriolis,
    )


def solution(mesh):
    placed = (
        P(None, "lon", "lat"),
        P("lon", "lat"),
        P(),
        P(),
        P("lon", "lat", None),
        P("lon", "lat", None),
        P(None, "lon", "lat"),
        P(None, "lon", "lat"),
        P("lon", "lat"),
        P("lat"),
    )
    return jax.shard_map(
        local,
        mesh=mesh,
        in_specs=placed,
        out_specs=(P(None, "lon", "lat"), P(None, "lon", "lat"), P(None, "lon", "lat")),
        check_vma=False,
    )
```

time: 142 us -> 86.6 us (0.61)
  Pallas kernels: 137 us -> 85.8 us
  local copies, waits for them, and re-layouts: 2.98 us -> 0 us
    pallas_call x4 -> x2, Pallas kernels: 137 us -> 85.8 us  [the longest x1 69.5 us: local(): pl.pallas_call(wave_kernel, name='wave', out_shape=(S((width, components,...]
where the time goes in v3:
time: 86.6 us; the launch traced here: 86.4 us
  Pallas kernels  85.8 us (99%)
    pallas_call x1, Pallas kernels, local(): pl.pallas_call(wave_kernel, name='wave', out_shape=(S((width, components,...  69.5 us
    pallas_call x1, Pallas kernels, local(): pl.pallas_call(ocean_kernel, name='ocean', out_shape=(S(spectrum.shape, f...  16.3 us

profile of v3, /device:TPU:1, one launch (start us, length us, event | category | flops | bytes accessed | tf_op | source)
XLA Modules:
  0.0 86.4 jit_solution(13881866533776980915)
XLA Ops:
  0.6 69.5 %wave.1 = (f32[8,1296,128]{2,1,0:T(8,128)}, f32[3,5,8,128]{3,2,1,0:T(8,128)}, f32[2,3,2,8,128]{4,3,2,1,0:T(8,128)}, f32[2,2,8,128]{3,2,1,0:T(8,128)}, s32[4,24,3...) custom-call(f32[1296,8,128]{2,1,0:T(8,128)} %spectrum.1, s32[8,128]{1,0:T(8,128)} %sea.2, ...), custom_call_target="tpu_custom_call" | custom-call | tf_op jit(solution)/shard_map/wave/pallas_call | solution.py:843
  70.1 16.3 %ocean.1 = (f32[1296,8,128]{2,1,0:T(8,128)}, f32[8,24,384]{2,1,0:T(8,128)}, f32[8,24,384]{2,1,0:T(8,128)}) custom-call(f32[8,1296,128]{2,1,0:T(8,128)} %get-tuple-element.11.s2, f32[3,5,8,128]{3,2,1,0:T(8,128)} %get-tuple-element.12.near, f32[2,3,2,8,128]{4,3,2,1,0:T(8,128)} %get-tuple-element.13.sides, f32[2,2,8,128]{3,2,1,0:T(8,128)} %get-tuple-element.14.far, ...), custom_call_target="tpu_custom_call" | custom-call | tf_op jit(solution)/shard_map/ocean/pallas_call | solution.py:902

commit v4 on v3

--- a/solution.py
+++ b/solution.py
@@ -12,9 +12,12 @@
 MESH = pl.DeviceIdType.MESH
 VMEM = pl.BlockSpec(memory_space=pltpu.VMEM)
 ANY = pl.BlockSpec(memory_space=pl.ANY)
+HBM = pl.BlockSpec(memory_space=pltpu.HBM)
 LANES = 128
 PAIR = 16
-GRANT = 60 * 1024 * 1024
+OCEAN_GRANT = 12000 * 1024
+WAVE_GRANT = 40000 * 1024
+HEAD = 176
 
 
 def courant(components, freqs):
@@ -32,6 +35,10 @@
     for d in range(first // freqs, (last - 1) // freqs + 1):
         signs.add(1 if function(2 * math.pi * (d + 0.5) / directions) > 0 else -1)
     return signs.pop() if len(signs) == 1 else 0
+
+
+def in_hbm(value):
+    return pltpu.with_memory_space_constraint(value, pltpu.HBM)
 
 
 def segments(components, freqs):
@@ -62,15 +69,9 @@
     return [tuple(s) for s in spans]
 
 
-def complement(spans, total):
-    out, at = [], 0
-    for a, b in spans:
-        if a > at:
-            out.append((at, a))
-        at = b
-    if at < total:
-        out.append((at, total))
-    return out
+def split(spans, rows):
+    a, b = spans[0]
+    return [(a, a + rows)], [(a + rows, b)] + list(spans[1:])
 
 
 def south_lane(c):
@@ -83,6 +84,10 @@
 
 def lane_shift(x, source, target):
     return pltpu.roll(x, (target - source) % LANES, 1)
+
+
+def lanes_of(x, index):
+    return jnp.take_along_axis(x, index, axis=1, mode="promise_in_bounds")
 
 
 def coefficients(coef, wide, r, xs, ys):
@@ -276,9 +281,14 @@
             for k0, k1 in spans
         ]
 
-    first = columns(
-        plus, lambda k: spectrum.at[k, width - 1, :], lambda k: x.at[1, k, :], east
-    ) + columns(minus, lambda k: spectrum.at[k, 0, :], lambda k: x.at[width + 2, k, :], west)
+    def first_columns(plus, minus):
+        return columns(
+            plus, lambda k: spectrum.at[k, width - 1, :], lambda k: x.at[1, k, :], east
+        ) + columns(minus, lambda k: spectrum.at[k, 0, :], lambda k: x.at[width + 2, k, :], west)
+
+    head, rest = zip(split(plus, HEAD), split(minus, HEAD))
+    first_head, first_rest = first_columns(*head), first_columns(*rest)
+    first = first_head + first_rest
     second = columns(
         plus, lambda k: a.at[width, k, :], lambda k: a.at[0, k, :], east
     ) + columns(minus, lambda k: a.at[1, k, :], lambda k: a.at[width + 1, k, :], west)
@@ -286,7 +296,7 @@
         remote(sea.at[pl.ds(width - 1, 1), :], far_masks.at[0], east, lat),
         remote(sea.at[pl.ds(0, 1), :], far_masks.at[1], west, lat),
     ]
-    for copy in side_masks + first:
+    for copy in side_masks + first_head:
         copy.start()
 
     for c in range(width):
@@ -297,12 +307,13 @@
     for copy in columns_in:
         copy.wait()
 
+    half = lane // 2
+    edge_lanes = jnp.where(half < 8, LANES - 2, 0) + lane % 2
+
     def pack(r, values):
         total = jnp.zeros((PAIR, LANES), jnp.float32)
-        half = lane // 2
         for c in range(width):
-            total = jnp.where(half == c, lane_shift(values[c], LANES - 2, 2 * c), total)
-            total = jnp.where(half == 8 + c, lane_shift(values[c], 0, 16 + 2 * c), total)
+            total = jnp.where(half % 8 == c, lanes_of(values[c], edge_lanes), total)
         packed[pl.ds(r, PAIR), :] = total
 
     def pack_rows(p):
@@ -346,6 +357,9 @@
     def _():
         for copy in to_south:
             copy.start()
+
+    for copy in first_rest:
+        copy.start()
 
     coef_in.wait()
     bulk_turned[...] = jnp.zeros_like(bulk_turned)
@@ -506,23 +520,6 @@
 
     for copy in side_masks + first:
         copy.wait_recv()
-    rows_copy = [
-        remote(rows_send.at[0], rows_in.at[0], east, lat),
-        remote(rows_send.at[1], rows_in.at[1], west, lat),
-    ]
-    cols_north = remote(cols_send.at[0], cols_in.at[0], lon, lat + 1)
-    cols_south = remote(cols_send.at[1], cols_in.at[1], lon, lat - 1)
-    for copy in rows_copy:
-        copy.start()
-
-    @pl.when(has_north)
-    def _():
-        cols_north.start()
-
-    @pl.when(has_south)
-    def _():
-        cols_south.start()
-
     for slot, side in ((1, 0), (width + 2, 1)):
         masks[slot] = jnp.broadcast_to(far_masks[side].astype(jnp.float32), (PAIR, LANES))
 
@@ -543,6 +540,22 @@
     outer_product(a, 1)
     for copy in second:
         copy.start()
+    rows_copy = [
+        remote(rows_send.at[0], rows_in.at[0], east, lat),
+        remote(rows_send.at[1], rows_in.at[1], west, lat),
+    ]
+    cols_north = remote(cols_send.at[0], cols_in.at[0], lon, lat + 1)
+    cols_south = remote(cols_send.at[1], cols_in.at[1], lon, lat - 1)
+    for copy in rows_copy:
+        copy.start()
+
+    @pl.when(has_north)
+    def _():
+        cols_north.start()
+
+    @pl.when(has_south)
+    def _():
+        cols_south.start()
 
     def second_step(group, target):
         def step(r, xs, ys):
@@ -651,34 +664,32 @@
 
 
 def taken_from(sources, codes, quantities):
-    places = [c & (LANES - 1) for c in codes]
-    offsets = [c >> 9 for c in codes]
-    taken = [[jnp.zeros(codes[0].shape, jnp.float32)] * len(quantities) for _ in codes]
-    for o in range(17):
-        hits = [offset == o for offset in offsets]
-        for n, q in enumerate(quantities):
-            source = sources(q, o)
-            for i in range(len(codes)):
-                got = jnp.take_along_axis(source, places[i], axis=1, mode="promise_in_bounds")
-                taken[i][n] = jnp.where(hits[i], got, taken[i][n])
+    taken = []
+    for code in codes:
+        place, offset = code & (LANES - 1), code >> 9
+        values = [jnp.zeros(code.shape, jnp.float32)] * len(quantities)
+        for o in range(17):
+            hit = offset == o
+            for n, q in enumerate(quantities):
+                values[n] = jnp.where(hit, lanes_of(sources(q, o), place), values[n])
+        taken.append(values)
     return taken
 
 
 def ocean_kernel(
-    s2, near, sides, far, cells, weights, rows_in, cols_in, u, v, sea, coriolis,
+    s2, u, v, sea, near, sides, far, cells, weights, rows_in, cols_in, coriolis,
     spectrum_out, u_out, v_out,
-    near1, near3, sides3, forcing, edge_code, edge_weight, edge_rows, state, in_sem, out_sem,
+    near1, near3, sides3, forcing, edge_code, edge_weight, edge_rows, out_sem,
 ):
     quantities = near.shape[1]
     width = near.shape[2]
     taps, height, length = cells.shape
     levels = u.shape[0]
-    reads = [pltpu.make_async_copy(s2.at[c], state.at[c], in_sem.at[c]) for c in range(width)]
     writes = [
-        pltpu.make_async_copy(state.at[c], spectrum_out.at[:, c, :], out_sem.at[c])
+        pltpu.make_async_copy(s2.at[c], spectrum_out.at[:, c, :], out_sem.at[c])
         for c in range(width)
     ]
-    for copy in reads:
+    for copy in writes:
         copy.start()
     for part in range(3):
         near1[:, pl.ds(8 + part * width, width), :] = near[part]
@@ -695,8 +706,8 @@
                     sides[side, i // width, q, pl.ds(i % width, 1), :], (3, LANES)
                 )
 
-    def block(jb, carry):
-        lanes = pl.ds(pl.multiple_of(jb * LANES, LANES), LANES)
+    def block(jb):
+        lanes = pl.ds(jb * LANES, LANES)
         for i0 in range(0, height, 8):
             rows = pl.ds(i0, 8)
             taken = taken_from(
@@ -728,15 +739,13 @@
             edge_rows[q, pl.ds(1, 1), lanes] = jnp.sum(
                 jnp.where(low, zero, product), axis=0, keepdims=True
             )
-        return carry
-
-    for read, write in zip(reads, writes):
-        read.wait()
-        write.start()
+
     for side in range(2):
         edge_code[pl.ds(4 * side, 4), :] = rows_in[side, pl.ds(2 * levels + taps, taps), :]
         edge_weight[pl.ds(4 * side, 4), :] = rows_in[side, pl.ds(2 * levels, taps), :]
-    lax.fori_loop(0, length // LANES, block, 0)
+    blocks = length // LANES
+    for jb in range(blocks):
+        block(jb)
 
     lane = lax.broadcasted_iota(jnp.int32, (8, LANES), 1)
     here = jnp.logical_and(lane >= 2 * levels + taps, lane < 2 * levels + 2 * taps)
@@ -853,7 +862,7 @@
             S((2, messages, length), f32),
             S((2, height, LANES), f32),
         ),
-        in_specs=[ANY, VMEM, ANY, ANY, VMEM, ANY, ANY, ANY, ANY],
+        in_specs=[HBM, VMEM, HBM, HBM, VMEM, HBM, HBM, HBM, HBM],
         out_specs=(ANY,) * 8,
         scratch_shapes=[
             pltpu.VMEM((width + 4, components, LANES), f32),
@@ -892,11 +901,16 @@
             dma((16,)),
         ],
         compiler_params=pltpu.CompilerParams(
-            collective_id=0, has_side_effects=True, vmem_limit_bytes=GRANT
+            collective_id=0, has_side_effects=True, vmem_limit_bytes=WAVE_GRANT
         ),
     )(
-        spectrum, sea_mask, transfer, jnp.asarray(coef), bulk_weight, cell, weight,
-        ocean_u, ocean_v,
+        *map(
+            in_hbm,
+            (
+                spectrum, sea_mask, transfer, jnp.asarray(coef), bulk_weight, cell, weight,
+                ocean_u, ocean_v,
+            ),
+        )
     )
 
     return pl.pallas_call(
@@ -904,7 +918,7 @@
         name="ocean",
         out_shape=(S(spectrum.shape, f32), S(ocean_u.shape, f32), S(ocean_v.shape, f32)),
         in_specs=[ANY] + [VMEM] * 11,
-        out_specs=(ANY, VMEM, VMEM),
+        out_specs=(HBM, VMEM, VMEM),
         scratch_shapes=[
             pltpu.VMEM((quantities, 8 + 3 * width + 8, LANES), f32),
             pltpu.VMEM((quantities, 9 * width, LANES), f32),
@@ -913,13 +927,11 @@
             pltpu.VMEM((8, length), f32),
             pltpu.VMEM((8, length), f32),
             pltpu.VMEM((2, 8, length), f32),
-            pltpu.VMEM((width, components, LANES), f32),
-            dma((width,)),
             dma((width,)),
         ],
-        compiler_params=pltpu.CompilerParams(vmem_limit_bytes=GRANT),
+        compiler_params=pltpu.CompilerParams(vmem_limit_bytes=OCEAN_GRANT),
     )(
-        s2, near, sides, far, cells, weights, rows_in, cols_in, ocean_u, ocean_v, ocean_mask,
+        s2, ocean_u, ocean_v, ocean_mask, near, sides, far, cells, weights, rows_in, cols_in,
         coriolis,
     )
 

time: 86.6 us -> 69.8 us (0.81)
  Pallas kernels: 85.8 us -> 68.8 us
    pallas_call x1, Pallas kernels: 16.3 us -> 7.43 us  [local(): pl.pallas_call(ocean_kernel, name='ocean', out_shape=(S(spectrum.shape, f...]
    pallas_call x1, Pallas kernels: 69.5 us -> 61.4 us  [local(): pl.pallas_call(wave_kernel, name='wave', out_shape=(S((width, components,...]
where the time goes in v4:
time: 69.8 us; the launch traced here: 69.7 us
  Pallas kernels  68.8 us (99%)
  between operations  0.87 us (1%)
    pallas_call x1, Pallas kernels, local(): pl.pallas_call(wave_kernel, name='wave', out_shape=(S((width, components,...  61.4 us
    pallas_call x1, Pallas kernels, local(): pl.pallas_call(ocean_kernel, name='ocean', out_shape=(S(spectrum.shape, f...  7.43 us

profile of v4, /device:TPU:1, one launch (start us, length us, event | category | flops | bytes accessed | tf_op | source)
XLA Modules:
  0.0 69.7 jit_solution(6269578807595352449)
XLA Ops:
  0.6 0.0 copy-start.1
  0.6 0.0 copy-start
  0.7 0.0 copy-start.3
  0.7 0.0 copy-start.2
  0.7 61.4 %wave.1 = (f32[8,1296,128]{2,1,0:T(8,128)S(1)}, f32[3,5,8,128]{3,2,1,0:T(8,128)S(1)}, f32[2,3,2,8,128]{4,3,2,1,0:T(8,128)S(1)}, f32[2,2,8,128]{3,2,1,0:T(8,128)S...) custom-call(f32[1296,8,128]{2,1,0:T(8,128)} %spectrum.1, ...), custom_call_target="tpu_custom_call" | custom-call | tf_op jit(solution)/shard_map/wave/pallas_call | solution.py:852
  62.1 0.0 copy-done.1
  62.1 0.0 copy-done
  62.1 0.0 copy-done.3
  62.1 0.0 copy-done.2
  62.1 7.4 %ocean.1 = (f32[1296,8,128]{2,1,0:T(8,128)}, f32[8,24,384]{2,1,0:T(8,128)}, f32[8,24,384]{2,1,0:T(8,128)}) custom-call(f32[8,1296,128]{2,1,0:T(8,128)S(1)} %get-tuple-element.11.s2, f32[8,24,384]{2,1,0:T(8,128)S(1)} %copy-done, f32[8,24,384]{2,1,0:T(8,128)S(1)} %copy-done.1, s32[24,384]{1,0:T(8,128)S(1)} %copy-done.2, ...), custom_call_target="tpu_custom_call" | custom-call | tf_op jit(solution)/shard_map/ocean/pallas_call | solution.py:916
Async XLA Ops:
  0.6 61.5 %copy-start.1 = (f32[8,24,384]{2,1,0:T(8,128)S(1)}, f32[8,24,384]{2,1,0:T(8,128)}, u32[]{:S(2)}) copy-start(f32[8,24,384]{2,1,0:T(8,128)} %v.1) | copy-start | bytes 884740
  0.6 61.5 %copy-start = (f32[8,24,384]{2,1,0:T(8,128)S(1)}, f32[8,24,384]{2,1,0:T(8,128)}, u32[]{:S(2)}) copy-start(f32[8,24,384]{2,1,0:T(8,128)} %u.1) | copy-start | bytes 884740
  0.7 61.5 %copy-start.3 = (f32[384]{0:T(512)S(1)}, f32[384]{0:T(512)}, u32[]{:S(2)}) copy-start(f32[384]{0:T(512)} %coriolis.1) | copy-start | bytes 4612
  0.7 61.5 %copy-start.2 = (s32[24,384]{1,0:T(8,128)S(1)}, s32[24,384]{1,0:T(8,128)}, u32[]{:S(2)}) copy-start(s32[24,384]{1,0:T(8,128)} %sea.3) | copy-start | bytes 110596

commit v5 on v4

--- a/solution.py
+++ b/solution.py
@@ -17,7 +17,7 @@
 PAIR = 16
 OCEAN_GRANT = 12000 * 1024
 WAVE_GRANT = 40000 * 1024
-HEAD = 176
+PARTS = (((0, 256), (384, 640)), ((640, 896), (1024, 1296)), ((256, 384), (896, 1024)))
 
 
 def courant(components, freqs):
@@ -69,9 +69,14 @@
     return [tuple(s) for s in spans]
 
 
-def split(spans, rows):
-    a, b = spans[0]
-    return [(a, a + rows)], [(a + rows, b)] + list(spans[1:])
+def overlap(spans, low, high):
+    cut = [(max(a, low), min(b, high)) for a, b in spans]
+    return [(a, b) for a, b in cut if a < b]
+
+
+def clipped(runs, low, high):
+    cut = [(max(a, low // PAIR), min(b, high // PAIR), xs, ys) for a, b, xs, ys in runs]
+    return [run for run in cut if run[0] < run[1]]
 
 
 def south_lane(c):
@@ -204,8 +209,8 @@
     spectrum, sea, transfer, coef_hbm, bulk_weight, cell_hbm, weight_hbm, u_hbm, v_hbm,
     s2_out, near_out, sides_out, far_out, cells_out, weights_out, rows_out, cols_out,
     x, a, ab, abe, t, coef, wide, bulk_turned, bulk_wide, masks, packed, turned, gturned, g, ga,
-    cell, weight, u, v, cells, weights, rows_send, cols_send, rows_in, cols_in,
-    bulk, near, sides, far, far_masks, local_sem, send_sem, recv_sem, out_sem,
+    cell, weight, u, v, cells, weights, rows_send, cols_send, cols_in,
+    bulk, far_masks, acc, local_sem, send_sem, recv_sem, out_sem,
 ):
     lon, lat = lax.axis_index("lon"), lax.axis_index("lat")
     nlon, nlat = lax.axis_size("lon"), lax.axis_size("lat")
@@ -221,7 +226,6 @@
 
     gturned[...] = jnp.zeros_like(gturned)
     cols_in[...] = jnp.zeros_like(cols_in)
-    sides[...] = jnp.zeros_like(sides)
 
     local = []
 
@@ -281,22 +285,38 @@
             for k0, k1 in spans
         ]
 
-    def first_columns(plus, minus):
-        return columns(
-            plus, lambda k: spectrum.at[k, width - 1, :], lambda k: x.at[1, k, :], east
-        ) + columns(minus, lambda k: spectrum.at[k, 0, :], lambda k: x.at[width + 2, k, :], west)
-
-    head, rest = zip(split(plus, HEAD), split(minus, HEAD))
-    first_head, first_rest = first_columns(*head), first_columns(*rest)
-    first = first_head + first_rest
-    second = columns(
-        plus, lambda k: a.at[width, k, :], lambda k: a.at[0, k, :], east
-    ) + columns(minus, lambda k: a.at[1, k, :], lambda k: a.at[width + 1, k, :], west)
+    def both_ways(part, east_source, east_target, west_source, west_target):
+        copies = []
+        for low, high in part:
+            copies += columns(overlap(plus, low, high), east_source, east_target, east)
+            copies += columns(overlap(minus, low, high), west_source, west_target, west)
+        return copies
+
+    first = [
+        both_ways(
+            part,
+            lambda k: spectrum.at[k, width - 1, :],
+            lambda k: x.at[1, k, :],
+            lambda k: spectrum.at[k, 0, :],
+            lambda k: x.at[width + 2, k, :],
+        )
+        for part in PARTS
+    ]
+    second = [
+        both_ways(
+            part,
+            lambda k: a.at[width, k, :],
+            lambda k: a.at[0, k, :],
+            lambda k: a.at[1, k, :],
+            lambda k: a.at[width + 1, k, :],
+        )
+        for part in PARTS
+    ]
     side_masks = [
         remote(sea.at[pl.ds(width - 1, 1), :], far_masks.at[0], east, lat),
         remote(sea.at[pl.ds(0, 1), :], far_masks.at[1], west, lat),
     ]
-    for copy in side_masks + first_head:
+    for copy in side_masks + first[0]:
         copy.start()
 
     for c in range(width):
@@ -358,7 +378,7 @@
         for copy in to_south:
             copy.start()
 
-    for copy in first_rest:
+    for copy in first[1] + first[2]:
         copy.start()
 
     coef_in.wait()
@@ -474,7 +494,6 @@
         ab[rows, ghost_at : ghost_at + LANES] = value.astype(jnp.bfloat16)
 
     over_rows(runs, first_inner)
-    transfer_in.wait()
     block = 432
     ghost_mask = g[pl.ds(components, 1), :]
 
@@ -503,22 +522,35 @@
 
         lax.fori_loop(0, components // block, product, 0)
 
-    def outer_product(state, shift):
+    def outer_part(index, advect_rows, state, shift):
+        part = PARTS[index]
+        for low, high in part:
+            over_rows(clipped(runs, low, high), advect_rows, 8)
+
         def product(m, carry):
             rows = pl.ds(pl.multiple_of(m * block, PAIR), block)
-            added = jnp.dot(t[rows, :], abe[...], preferred_element_type=jnp.float32)
-            for n, c in enumerate(outer):
-                part = added[:, n * LANES : (n + 1) * LANES]
-                state[c + shift, rows, :] = masks[c + 2, pl.ds(0, 1), :] * (
-                    state[c + shift, rows, :] + 0.5 * part
+            added = sum(
+                jnp.dot(
+                    t[rows, low:high], abe[low:high, :], preferred_element_type=jnp.float32
                 )
+                for low, high in part
+            )
+            if index:
+                added = added + acc[rows, :]
+            if index < len(PARTS) - 1:
+                acc[rows, :] = added
+            else:
+                for n, c in enumerate(outer):
+                    wet = masks[c + 2, pl.ds(0, 1), :]
+                    state[c + shift, rows, :] = wet * (
+                        state[c + shift, rows, :] + 0.5 * added[:, n * LANES : (n + 1) * LANES]
+                    )
             return carry
 
         lax.fori_loop(0, components // block, product, 0)
 
-    inner_product(a, 1, True)
-
-    for copy in side_masks + first:
+
+    for copy in side_masks:
         copy.wait_recv()
     for slot, side in ((1, 0), (width + 2, 1)):
         masks[slot] = jnp.broadcast_to(far_masks[side].astype(jnp.float32), (PAIR, LANES))
@@ -536,13 +568,17 @@
             a[c + 1, rows, :] = value
             abe[rows, n * LANES : (n + 1) * LANES] = value.astype(jnp.bfloat16)
 
-    over_rows(runs, first_outer)
-    outer_product(a, 1)
-    for copy in second:
-        copy.start()
+    transfer_in.wait()
+    for index, copies in enumerate(first):
+        for copy in copies:
+            copy.wait_recv()
+        outer_part(index, first_outer, a, 1)
+    for copies in second:
+        for copy in copies:
+            copy.start()
     rows_copy = [
-        remote(rows_send.at[0], rows_in.at[0], east, lat),
-        remote(rows_send.at[1], rows_in.at[1], west, lat),
+        remote(rows_send.at[0], rows_out.at[0], east, lat),
+        remote(rows_send.at[1], rows_out.at[1], west, lat),
     ]
     cols_north = remote(cols_send.at[0], cols_in.at[0], lon, lat + 1)
     cols_south = remote(cols_send.at[1], cols_in.at[1], lon, lat - 1)
@@ -556,6 +592,8 @@
     @pl.when(has_south)
     def _():
         cols_south.start()
+
+    inner_product(a, 1, True)
 
     def second_step(group, target):
         def step(r, xs, ys):
@@ -568,20 +606,21 @@
                 x[c + 2, rows, :] = value
                 target[rows, n * LANES : (n + 1) * LANES] = value.astype(jnp.bfloat16)
 
-        over_rows(runs, step)
-
-    for copy in side_masks + first:
-        copy.wait_send()
-    second_step(inner, ab)
+        return step
+
+    for copies in [side_masks] + first:
+        for copy in copies:
+            copy.wait_send()
+    over_rows(runs, second_step(inner, ab))
     inner_product(x, 2, False)
     for c in inner:
         store(x.at[c + 2], s2_out.at[c])
     bulk_of(bulk_wide, x, inner, quantities, components, bulk)
 
-    for copy in second:
-        copy.wait_recv()
-    second_step(outer, abe)
-    outer_product(x, 2)
+    for index, copies in enumerate(second):
+        for copy in copies:
+            copy.wait_recv()
+        outer_part(index, second_step(outer, abe), x, 2)
     for c in outer:
         store(x.at[c + 2], s2_out.at[c])
     bulk_of(bulk_wide, x, outer, quantities, components, bulk)
@@ -589,20 +628,20 @@
     drift = bulk.at[pl.ds(1, 2)]
     stress = bulk.at[pl.ds(0, 2)]
     flat = [
-        remote(bulk, near.at[2], west, lat),
-        remote(bulk, near.at[0], east, lat),
-        remote(stress, far.at[1], around[0], lat),
-        remote(stress, far.at[0], around[4], lat),
+        remote(bulk, near_out.at[2], west, lat),
+        remote(bulk, near_out.at[0], east, lat),
+        remote(stress, far_out.at[1], around[0], lat),
+        remote(stress, far_out.at[0], around[4], lat),
     ]
     spread_north = [
-        remote(drift, sides.at[0, 2], west, lat + 1),
-        remote(drift, sides.at[0, 1], lon, lat + 1),
-        remote(drift, sides.at[0, 0], east, lat + 1),
+        remote(drift, sides_out.at[0, 2], west, lat + 1),
+        remote(drift, sides_out.at[0, 1], lon, lat + 1),
+        remote(drift, sides_out.at[0, 0], east, lat + 1),
     ]
     spread_south = [
-        remote(drift, sides.at[1, 2], west, lat - 1),
-        remote(drift, sides.at[1, 1], lon, lat - 1),
-        remote(drift, sides.at[1, 0], east, lat - 1),
+        remote(drift, sides_out.at[1, 2], west, lat - 1),
+        remote(drift, sides_out.at[1, 1], lon, lat - 1),
+        remote(drift, sides_out.at[1, 0], east, lat - 1),
     ]
     for copy in flat:
         copy.start()
@@ -617,12 +656,13 @@
         for copy in spread_south:
             copy.start()
 
-    near[1] = bulk[...]
+    store(bulk, near_out.at[1])
 
     for copy in rows_copy:
         copy.wait()
-    for copy in second:
-        copy.wait_send()
+    for copies in second:
+        for copy in copies:
+            copy.wait_send()
 
     @pl.when(has_north)
     def _():
@@ -636,7 +676,6 @@
             copy.wait_send()
         cols_north.wait_recv()
 
-    store(rows_in, rows_out)
     store(cols_in, cols_out)
 
     for copy in flat:
@@ -656,9 +695,6 @@
         for copy in spread_north:
             copy.wait_recv()
 
-    store(near, near_out)
-    store(sides, sides_out)
-    store(far, far_out)
     for copy in stores:
         copy.wait()
 
@@ -679,7 +715,7 @@
 def ocean_kernel(
     s2, u, v, sea, near, sides, far, cells, weights, rows_in, cols_in, coriolis,
     spectrum_out, u_out, v_out,
-    near1, near3, sides3, forcing, edge_code, edge_weight, edge_rows, out_sem,
+    near1, near3, sides3, forcing, edge_code, edge_weight, edge_rows, new_u, new_v, out_sem,
 ):
     quantities = near.shape[1]
     width = near.shape[2]
@@ -750,6 +786,8 @@
     lane = lax.broadcasted_iota(jnp.int32, (8, LANES), 1)
     here = jnp.logical_and(lane >= 2 * levels + taps, lane < 2 * levels + 2 * taps)
     edge_cols = [[], []]
+    lat = lax.axis_index("lat")
+    present = (lat > 0, lat < lax.axis_size("lat") - 1)
     for side in range(2):
         parts = [[], []]
         for i0 in range(0, height, 8):
@@ -760,7 +798,8 @@
             )
             weight = jnp.where(here, pltpu.roll(line, taps, 1), 0.0)
             for q in range(2):
-                parts[q].append(jnp.sum(taken[0][q] * weight, axis=1, keepdims=True))
+                value = jnp.sum(taken[0][q] * weight, axis=1, keepdims=True)
+                parts[q].append(jnp.where(present[side], value, 0.0))
         for q in range(2):
             edge_cols[side].append(jnp.concatenate(parts[q], axis=0))
 
@@ -806,18 +845,24 @@
             )
             return east + west + north + south - 4.0 * q
 
-        u_out[level] = wet * (
+        new_u[level] = wet * (
             here_u
             + turn * (here_v + decay * forcing[4])
             + (0.5 * decay) * force_x
             + 0.1 * laplace(here_u, level)
         )
-        v_out[level] = wet * (
+        new_v[level] = wet * (
             here_v
             - turn * (here_u + decay * forcing[3])
             + (0.5 * decay) * force_y
             + 0.1 * laplace(here_v, levels + level)
         )
+        for n, (src, dst) in enumerate(((new_u, u_out), (new_v, v_out))):
+            copy = pltpu.make_async_copy(
+                src.at[level], dst.at[level], out_sem.at[width + n * levels + level]
+            )
+            copy.start()
+            writes.append(copy)
     for copy in writes:
         copy.wait()
 
@@ -888,16 +933,13 @@
             pltpu.VMEM((taps, height, length), f32),
             pltpu.VMEM((2, messages, length), f32),
             pltpu.VMEM((2, height, LANES), f32),
-            pltpu.VMEM((2, messages, length), f32),
             pltpu.VMEM((2, height, LANES), f32),
             pltpu.VMEM((quantities, width, LANES), f32),
-            pltpu.VMEM(near_shape, f32),
-            pltpu.VMEM(sides_shape, f32),
-            pltpu.VMEM(far_shape, f32),
             pltpu.VMEM((2, 1, LANES), i32),
+            pltpu.VMEM((components, 2 * LANES), f32),
             dma((16,)),
-            dma((32,)),
-            dma((32,)),
+            dma((40,)),
+            dma((40,)),
             dma((16,)),
         ],
         compiler_params=pltpu.CompilerParams(
@@ -918,7 +960,7 @@
         name="ocean",
         out_shape=(S(spectrum.shape, f32), S(ocean_u.shape, f32), S(ocean_v.shape, f32)),
         in_specs=[ANY] + [VMEM] * 11,
-        out_specs=(HBM, VMEM, VMEM),
+        out_specs=(HBM, HBM, HBM),
         scratch_shapes=[
             pltpu.VMEM((quantities, 8 + 3 * width + 8, LANES), f32),
             pltpu.VMEM((quantities, 9 * width, LANES), f32),
@@ -927,7 +969,9 @@
             pltpu.VMEM((8, length), f32),
             pltpu.VMEM((8, length), f32),
             pltpu.VMEM((2, 8, length), f32),
-            dma((width,)),
+            pltpu.VMEM(ocean_u.shape, f32),
+            pltpu.VMEM(ocean_v.shape, f32),
+            dma((width + 2 * levels,)),
         ],
         compiler_params=pltpu.CompilerParams(vmem_limit_bytes=OCEAN_GRANT),
     )(

time: 69.8 us -> 66.7 us (0.956)
  Pallas kernels: 68.8 us -> 65.7 us
    pallas_call x1, Pallas kernels: 61.4 us -> 58.7 us  [local(): pl.pallas_call(wave_kernel, name='wave', out_shape=(S((width, components,...]
where the time goes in v5:
time: 66.7 us; the launch traced here: 66.6 us
  Pallas kernels  65.7 us (99%)
  between operations  0.87 us (1%)
    pallas_call x1, Pallas kernels, local(): pl.pallas_call(wave_kernel, name='wave', out_shape=(S((width, components,...  58.7 us
    pallas_call x1, Pallas kernels, local(): pl.pallas_call(ocean_kernel, name='ocean', out_shape=(S(spectrum.shape, f...  7.02 us

profile of v5, /device:TPU:1, one launch (start us, length us, event | category | flops | bytes accessed | tf_op | source)
XLA Modules:
  0.0 66.6 jit_solution(11723030700789701336)
XLA Ops:
  0.6 0.0 copy-start.1
  0.6 0.0 copy-start
  0.7 0.0 copy-start.3
  0.7 0.0 copy-start.2
  0.7 58.7 %wave.1 = (f32[8,1296,128]{2,1,0:T(8,128)S(1)}, f32[3,5,8,128]{3,2,1,0:T(8,128)S(1)}, f32[2,3,2,8,128]{4,3,2,1,0:T(8,128)S(1)}, f32[2,2,8,128]{3,2,1,0:T(8,128)S...) custom-call(f32[1296,8,128]{2,1,0:T(8,128)} %spectrum.1, ...), custom_call_target="tpu_custom_call" | custom-call | tf_op jit(solution)/shard_map/wave/pallas_call | solution.py:897
  59.4 0.0 copy-done.1
  59.4 0.0 copy-done
  59.4 0.0 copy-done.3
  59.4 0.0 copy-done.2
  59.4 7.0 %ocean.1 = (f32[1296,8,128]{2,1,0:T(8,128)}, f32[8,24,384]{2,1,0:T(8,128)}, f32[8,24,384]{2,1,0:T(8,128)}) custom-call(f32[8,1296,128]{2,1,0:T(8,128)S(1)} %get-tuple-element.11.s2, f32[8,24,384]{2,1,0:T(8,128)S(1)} %copy-done, f32[8,24,384]{2,1,0:T(8,128)S(1)} %copy-done.1, s32[24,384]{1,0:T(8,128)S(1)} %copy-done.2, ...), custom_call_target="tpu_custom_call" | custom-call | tf_op jit(solution)/shard_map/ocean/pallas_call | solution.py:958
Async XLA Ops:
  0.6 58.8 %copy-start.1 = (f32[8,24,384]{2,1,0:T(8,128)S(1)}, f32[8,24,384]{2,1,0:T(8,128)}, u32[]{:S(2)}) copy-start(f32[8,24,384]{2,1,0:T(8,128)} %v.1) | copy-start | bytes 884740
  0.6 58.8 %copy-start = (f32[8,24,384]{2,1,0:T(8,128)S(1)}, f32[8,24,384]{2,1,0:T(8,128)}, u32[]{:S(2)}) copy-start(f32[8,24,384]{2,1,0:T(8,128)} %u.1) | copy-start | bytes 884740
  0.7 58.8 %copy-start.3 = (f32[384]{0:T(512)S(1)}, f32[384]{0:T(512)}, u32[]{:S(2)}) copy-start(f32[384]{0:T(512)} %coriolis.1) | copy-start | bytes 4612
  0.7 58.8 %copy-start.2 = (s32[24,384]{1,0:T(8,128)S(1)}, s32[24,384]{1,0:T(8,128)}, u32[]{:S(2)}) copy-start(s32[24,384]{1,0:T(8,128)} %sea.3) | copy-start | bytes 110596

commit v6 on v5

--- a/solution.py
+++ b/solution.py
@@ -1,3 +1,4 @@
+import functools
 import math
 
 import jax
@@ -18,6 +19,9 @@
 OCEAN_GRANT = 12000 * 1024
 WAVE_GRANT = 40000 * 1024
 PARTS = (((0, 256), (384, 640)), ((640, 896), (1024, 1296)), ((256, 384), (896, 1024)))
+LAST = sum(high - low for low, high in PARTS[-1])
+HEAD = ((0, 128), (384, 512))
+BEHIND = ((128, 256), (512, 640))
 
 
 def courant(components, freqs):
@@ -210,7 +214,7 @@
     s2_out, near_out, sides_out, far_out, cells_out, weights_out, rows_out, cols_out,
     x, a, ab, abe, t, coef, wide, bulk_turned, bulk_wide, masks, packed, turned, gturned, g, ga,
     cell, weight, u, v, cells, weights, rows_send, cols_send, cols_in,
-    bulk, far_masks, acc, local_sem, send_sem, recv_sem, out_sem,
+    bulk, far_masks, acc, tl, abl, local_sem, send_sem, recv_sem, out_sem,
 ):
     lon, lat = lax.axis_index("lon"), lax.axis_index("lat")
     nlon, nlat = lax.axis_size("lon"), lax.axis_size("lat")
@@ -300,7 +304,7 @@
             lambda k: spectrum.at[k, 0, :],
             lambda k: x.at[width + 2, k, :],
         )
-        for part in PARTS
+        for part in (HEAD, BEHIND) + PARTS[1:]
     ]
     second = [
         both_ways(
@@ -378,7 +382,7 @@
         for copy in to_south:
             copy.start()
 
-    for copy in first[1] + first[2]:
+    for copy in first[1] + first[2] + first[3]:
         copy.start()
 
     coef_in.wait()
@@ -497,7 +501,7 @@
     block = 432
     ghost_mask = g[pl.ds(components, 1), :]
 
-    def inner_product(state, shift, with_ghost):
+    def inner_product(state, shift, with_ghost, begin, end):
         def product(m, carry):
             rows = pl.ds(pl.multiple_of(m * block, PAIR), block)
             for n in range(0, len(inner), 2):
@@ -520,42 +524,43 @@
                 ga[rows, :] = ghost_mask * (ga[rows, :] + 0.5 * added)
             return carry
 
-        lax.fori_loop(0, components // block, product, 0)
+        lax.fori_loop(begin, end, product, 0)
 
     def outer_part(index, advect_rows, state, shift):
-        part = PARTS[index]
-        for low, high in part:
-            over_rows(clipped(runs, low, high), advect_rows, 8)
-
-        def product(m, carry):
-            rows = pl.ds(pl.multiple_of(m * block, PAIR), block)
-            added = sum(
-                jnp.dot(
-                    t[rows, low:high], abe[low:high, :], preferred_element_type=jnp.float32
+        last = index == len(PARTS) - 1
+        at = 0
+        for low, high in PARTS[index]:
+            target, moved = (abl, at - low) if last else (abe, 0)
+            over_rows(
+                clipped(runs, low, high), functools.partial(advect_rows, target, moved), 8
+            )
+            at += high - low
+        for m in range(components // block):
+            rows = pl.ds(m * block, block)
+            if last:
+                added = acc[rows, :] + jnp.dot(
+                    tl[rows, :], abl[...], preferred_element_type=jnp.float32
                 )
-                for low, high in part
-            )
-            if index:
-                added = added + acc[rows, :]
-            if index < len(PARTS) - 1:
-                acc[rows, :] = added
-            else:
                 for n, c in enumerate(outer):
                     wet = masks[c + 2, pl.ds(0, 1), :]
                     state[c + shift, rows, :] = wet * (
                         state[c + shift, rows, :] + 0.5 * added[:, n * LANES : (n + 1) * LANES]
                     )
-            return carry
-
-        lax.fori_loop(0, components // block, product, 0)
-
+            else:
+                added = sum(
+                    jnp.dot(
+                        t[rows, low:high], abe[low:high, :], preferred_element_type=jnp.float32
+                    )
+                    for low, high in PARTS[index]
+                )
+                acc[rows, :] = added + acc[rows, :] if index else added
 
     for copy in side_masks:
         copy.wait_recv()
     for slot, side in ((1, 0), (width + 2, 1)):
         masks[slot] = jnp.broadcast_to(far_masks[side].astype(jnp.float32), (PAIR, LANES))
 
-    def first_outer(r, xs, ys):
+    def first_outer(target, moved, r, xs, ys):
         co = coefficients(coef, wide, r, xs, ys)
         rows = pl.ds(r, PAIR)
         state = {}
@@ -566,10 +571,17 @@
             advect_columns(co, xs, ys, outer, state, g[rows, :], lane).items()
         ):
             a[c + 1, rows, :] = value
-            abe[rows, n * LANES : (n + 1) * LANES] = value.astype(jnp.bfloat16)
+            target[pl.ds(r + moved, PAIR), n * LANES : (n + 1) * LANES] = value.astype(
+                jnp.bfloat16
+            )
 
     transfer_in.wait()
-    for index, copies in enumerate(first):
+    at = 0
+    for low, high in PARTS[-1]:
+        tl[:, at : at + high - low] = t[:, low:high]
+        at += high - low
+    inner_product(a, 1, True, 0, 2)
+    for index, copies in enumerate((first[0] + first[1], first[2], first[3])):
         for copy in copies:
             copy.wait_recv()
         outer_part(index, first_outer, a, 1)
@@ -593,10 +605,10 @@
     def _():
         cols_south.start()
 
-    inner_product(a, 1, True)
-
-    def second_step(group, target):
-        def step(r, xs, ys):
+    inner_product(a, 1, True, 2, components // block)
+
+    def second_step(group):
+        def step(target, moved, r, xs, ys):
             co = coefficients(coef, wide, r, xs, ys)
             rows = pl.ds(r, PAIR)
             state = {c: a[c + 1, rows, :] for c in needed(group, xs)}
@@ -604,15 +616,17 @@
                 advect_columns(co, xs, ys, group, state, ga[rows, :], lane).items()
             ):
                 x[c + 2, rows, :] = value
-                target[rows, n * LANES : (n + 1) * LANES] = value.astype(jnp.bfloat16)
+                target[pl.ds(r + moved, PAIR), n * LANES : (n + 1) * LANES] = value.astype(
+                    jnp.bfloat16
+                )
 
         return step
 
     for copies in [side_masks] + first:
         for copy in copies:
             copy.wait_send()
-    over_rows(runs, second_step(inner, ab))
-    inner_product(x, 2, False)
+    over_rows(runs, functools.partial(second_step(inner), ab, 0))
+    inner_product(x, 2, False, 0, components // block)
     for c in inner:
         store(x.at[c + 2], s2_out.at[c])
     bulk_of(bulk_wide, x, inner, quantities, components, bulk)
@@ -620,7 +634,7 @@
     for index, copies in enumerate(second):
         for copy in copies:
             copy.wait_recv()
-        outer_part(index, second_step(outer, abe), x, 2)
+        outer_part(index, second_step(outer), x, 2)
     for c in outer:
         store(x.at[c + 2], s2_out.at[c])
     bulk_of(bulk_wide, x, outer, quantities, components, bulk)
@@ -937,9 +951,11 @@
             pltpu.VMEM((quantities, width, LANES), f32),
             pltpu.VMEM((2, 1, LANES), i32),
             pltpu.VMEM((components, 2 * LANES), f32),
+            pltpu.VMEM((components, LAST), jnp.bfloat16),
+            pltpu.VMEM((LAST, 2 * LANES), jnp.bfloat16),
             dma((16,)),
-            dma((40,)),
-            dma((40,)),
+            dma((44,)),
+            dma((44,)),
             dma((16,)),
         ],
         compiler_params=pltpu.CompilerParams(

time: 66.7 us -> 66 us (0.990)
  Pallas kernels: 65.7 us -> 65 us
    pallas_call x1, Pallas kernels: 58.7 us -> 58 us  [local(): pl.pallas_call(wave_kernel, name='wave', out_shape=(S((width, components,...]
where the time goes in v6:
time: 66 us; the launch traced here: 65.9 us
  Pallas kernels  65 us (98%)
  between operations  0.87 us (1%)
    pallas_call x1, Pallas kernels, local(): pl.pallas_call(wave_kernel, name='wave', out_shape=(S((width, components,...  58 us
    pallas_call x1, Pallas kernels, local(): pl.pallas_call(ocean_kernel, name='ocean', out_shape=(S(spectrum.shape, f...  7.02 us

profile of v6, /device:TPU:1, one launch (start us, length us, event | category | flops | bytes accessed | tf_op | source)
XLA Modules:
  0.0 65.9 jit_solution(10500688505557467676)
XLA Ops:
  0.6 0.0 copy-start.1
  0.6 0.0 copy-start
  0.7 0.0 copy-start.3
  0.7 0.0 copy-start.2
  0.7 58.0 %wave.1 = (f32[8,1296,128]{2,1,0:T(8,128)S(1)}, f32[3,5,8,128]{3,2,1,0:T(8,128)S(1)}, f32[2,3,2,8,128]{4,3,2,1,0:T(8,128)S(1)}, f32[2,2,8,128]{3,2,1,0:T(8,128)S...) custom-call(f32[1296,8,128]{2,1,0:T(8,128)} %spectrum.1, ...), custom_call_target="tpu_custom_call" | custom-call | tf_op jit(solution)/shard_map/wave/pallas_call | solution.py:911
  58.6 0.0 copy-done.1
  58.7 0.0 copy-done
  58.7 0.0 copy-done.3
  58.7 0.0 copy-done.2
  58.7 7.0 %ocean.1 = (f32[1296,8,128]{2,1,0:T(8,128)}, f32[8,24,384]{2,1,0:T(8,128)}, f32[8,24,384]{2,1,0:T(8,128)}) custom-call(f32[8,1296,128]{2,1,0:T(8,128)S(1)} %get-tuple-element.11.s2, f32[8,24,384]{2,1,0:T(8,128)S(1)} %copy-done, f32[8,24,384]{2,1,0:T(8,128)S(1)} %copy-done.1, s32[24,384]{1,0:T(8,128)S(1)} %copy-done.2, ...), custom_call_target="tpu_custom_call" | custom-call | tf_op jit(solution)/shard_map/ocean/pallas_call | solution.py:974
Async XLA Ops:
  0.6 58.0 %copy-start.1 = (f32[8,24,384]{2,1,0:T(8,128)S(1)}, f32[8,24,384]{2,1,0:T(8,128)}, u32[]{:S(2)}) copy-start(f32[8,24,384]{2,1,0:T(8,128)} %v.1) | copy-start | bytes 884740
  0.6 58.0 %copy-start = (f32[8,24,384]{2,1,0:T(8,128)S(1)}, f32[8,24,384]{2,1,0:T(8,128)}, u32[]{:S(2)}) copy-start(f32[8,24,384]{2,1,0:T(8,128)} %u.1) | copy-start | bytes 884740
  0.7 58.0 %copy-start.3 = (f32[384]{0:T(512)S(1)}, f32[384]{0:T(512)}, u32[]{:S(2)}) copy-start(f32[384]{0:T(512)} %coriolis.1) | copy-start | bytes 4612
  0.7 58.0 %copy-start.2 = (s32[24,384]{1,0:T(8,128)S(1)}, s32[24,384]{1,0:T(8,128)}, u32[]{:S(2)}) copy-start(s32[24,384]{1,0:T(8,128)} %sea.3) | copy-start | bytes 110596
